TPU v7x, 256 devices: a whole 4x4x8 slice. The times are simulated.
256 devices in a mesh: rows: 64 (over y, x_hi, z), tgt: 4 (over x_lo, core).
Axes of the slice: x: 4 (x_hi: 2, x_lo: 2; x = x_hi * 2 + x_lo), y: 4, z: 8, core: 2. Of those that a mesh axis runs over, the one named last changes fastest.
Arguments:
- frames: bfloat16 [512, 256, 128], P('rows', 'tgt'), may hold values from -8 to 8
- window: int32 [64, 3], P('rows'), may hold values from 0 to 1, as said below
- patch_embed_weight: bfloat16 [64, 128], replicated, may hold values from -0.75 to 0.75
- dilated_conv_weight: bfloat16 [9, 128, 128], replicated, may hold values from -0.1875 to 0.1875
- context_gate_weight: bfloat16 [128, 384], replicated, may hold values from -0.1875 to 0.1875
- hidden_gate_weight: bfloat16 [9, 128, 256], replicated, may hold values from -0.25 to 0.25
- candidate_weight: bfloat16 [128, 128], replicated, may hold values from -1 to 1
- motion_gate_weight: float32 [2, 384], replicated, may hold values from -0.75 to 0.75
- motion_head_weight: float32 [128, 2], replicated, may hold values from -0.5 to 0.5
Outputs:
- motion: float32 [2, 512, 256], P(None, 'rows', 'tgt')
- hidden: bfloat16 [512, 256, 128], P('rows', 'tgt')
Inputs may be any that keep to these rules, and one draw needn't show every extreme that they name: `window`: entry o of a band's row says whether target band (band + o - 1) is searched; the middle entry is always 1.
All inputs are finite; a program needn't handle non-finite values.
Results may differ from a plain program's by a relative error of at most 0.015.
The roundings to bfloat16 on the way count: a program that leaves them out, or rounds other values in their place, can miss the bound.
Values may be sent and summed in bfloat16 or wider, within the bound.
A program may use at most 64 MiB of HBM per device.

v0:
```python
import math

import jax
import jax.numpy as jnp
from jax import lax
from jax.sharding import PartitionSpec as P

ITERS = 3


def extended(x, sides, width):
    for axis, dim in sides:
        size, length = (lax.axis_size(axis), x.shape[dim])
        up = [(i, (i + 1) % size) for i in range(size - 1)]
        down = [(j, i) for i, j in up]
        last = lax.slice_in_dim(x, length - width, length, axis=dim)
        initial = lax.slice_in_dim(x, 0, width, axis=dim)
        before = lax.ppermute(last, axis, up)
        after = lax.ppermute(initial, axis, down)
        x = jnp.concatenate([before, x, after], axis=dim)
    return x


def passed_along(block, axis, distance):
    devices = range(lax.axis_size(axis))
    route = [(i - distance, i) for i in devices if i - distance in devices]
    return lax.ppermute(block, axis, route)


def kernel_tap_sum(padded_features, weights, grid_height, grid_width, stride):
    summed_taps = None
    for row_tap in range(3):
        for col_tap in range(3):
            tap_piece = padded_features[
                ...,
                stride * row_tap : stride * row_tap + grid_height,
                stride * col_tap : stride * col_tap + grid_width,
                :,
            ]
            tap_term = jnp.dot(
                tap_piece, weights[3 * row_tap + col_tap], preferred_element_type=jnp.float32
            )
            summed_taps = tap_term if summed_taps is None else summed_taps + tap_term
    return summed_taps


def band_scores(source, targets, score_scale):
    return (
        lax.dot_general(
            source, targets, (((1,), (1,)), ((), ())), preferred_element_type=jnp.float32
        )
        * score_scale
    )


def on_device(
    frames,
    window,
    patch_embed_weight,
    dilated_conv_weight,
    context_gate_weight,
    hidden_gate_weight,
    candidate_weight,
    motion_gate_weight,
    motion_head_weight,
):
    band_height, dilated_width = (frames.shape[0], frames.shape[1])
    half_width = frames.shape[2] // 2
    channels = patch_embed_weight.shape[1]
    hidden_w = candidate_weight.shape[0]
    first_frame = jnp.dot(
        frames[:, :, :half_width], patch_embed_weight, preferred_element_type=jnp.float32
    )
    second_frame = jnp.dot(
        frames[:, :, half_width:], patch_embed_weight, preferred_element_type=jnp.float32
    )
    encoded_frames = jnp.stack([first_frame, second_frame]).astype(jnp.bfloat16)
    rimmed_features = extended(encoded_frames, (("rows", 1), ("tgt", 2)), 2)
    feature_maps = (
        encoded_frames.astype(jnp.float32)
        + jax.nn.relu(
            kernel_tap_sum(rimmed_features, dilated_conv_weight, band_height, dilated_width, 2)
        )
    ).astype(jnp.bfloat16)
    context = feature_maps[0]
    target = feature_maps[1]
    wide_band = lax.all_gather(target, "tgt", axis=1, tiled=True)
    upper_wide = passed_along(wide_band, "rows", 1)
    lower_wide = passed_along(wide_band, "rows", -1)
    gathered = jnp.stack([upper_wide, wide_band, lower_wide])
    width_t = gathered.shape[2]
    targets = gathered.reshape(3, band_height * width_t, channels)
    source = context.reshape(band_height * dilated_width, channels)
    score_scale = 1.0 / math.sqrt(channels)
    band_index = lax.axis_index("rows")
    band_count = lax.axis_size("rows")
    offsets = jnp.arange(3, dtype=jnp.int32) - 1
    neighbour = band_index + offsets
    allowed = (window[0] == 1) & (neighbour >= 0) & (neighbour < band_count)
    row_peaks = []
    masses = []
    for offset_slot in range(3):
        scores = band_scores(source, targets[offset_slot], score_scale)
        row_top = jnp.max(scores, axis=1)
        row_peaks.append(jnp.where(allowed[offset_slot], row_top, -jnp.inf))
        masses.append(jnp.sum(jnp.exp(scores - row_top[:, None]), axis=1))
    largest = jnp.maximum(jnp.maximum(row_peaks[0], row_peaks[1]), row_peaks[2])
    row_total = jnp.zeros(largest.shape, jnp.float32)
    for offset_slot in range(3):
        row_total = row_total + jnp.where(
            allowed[offset_slot],
            masses[offset_slot] * jnp.exp(row_peaks[offset_slot] - largest),
            0.0,
        )
    row_pot = -(largest + jnp.log(row_total))
    col_peaks = []
    col_masses = []
    for offset_slot in range(3):
        shifted = band_scores(source, targets[offset_slot], score_scale) + row_pot[:, None]
        col_top = jnp.max(shifted, axis=0)
        col_peaks.append(col_top)
        col_masses.append(jnp.sum(jnp.exp(shifted - col_top[None, :]), axis=0))
    col_peak = jnp.stack(col_peaks)
    col_sum = jnp.stack(col_masses)
    top_all = lax.pmax(col_peak, "tgt")
    sum_all = lax.psum(col_sum * jnp.exp(col_peak - top_all), "tgt")
    col_pot = -(top_all + jnp.log(sum_all))
    target_cells = jnp.arange(band_height * width_t, dtype=jnp.int32)
    coords = jnp.stack(
        [
            (target_cells // width_t).astype(jnp.float32),
            (target_cells % width_t).astype(jnp.float32),
        ],
        axis=1,
    )
    source_cells = jnp.arange(band_height * dilated_width, dtype=jnp.int32)
    col_base = lax.axis_index("tgt") * dilated_width
    own_coords = jnp.stack(
        [
            (source_cells // dilated_width).astype(jnp.float32),
            (source_cells % dilated_width + col_base).astype(jnp.float32),
        ],
        axis=1,
    )
    weight_sum = jnp.zeros((band_height * dilated_width,), jnp.float32)
    moment = jnp.zeros((band_height * dilated_width, 2), jnp.float32)
    for offset_slot in range(3):
        exponent = (
            band_scores(source, targets[offset_slot], score_scale)
            + row_pot[:, None]
            + col_pot[offset_slot][None, :]
        )
        coupling = jnp.where(allowed[offset_slot], jnp.exp(exponent), 0.0)
        row_mass = jnp.sum(coupling, axis=1)
        weight_sum = weight_sum + row_mass
        row_offset = jnp.float32((offset_slot - 1) * band_height)
        moment = moment + jnp.dot(coupling, coords, precision=lax.Precision.HIGHEST)
        moment = moment.at[:, 0].add(row_offset * row_mass)
    relative = moment / weight_sum[:, None] - own_coords
    motion = jnp.transpose(relative.reshape(band_height, dilated_width, 2), (2, 0, 1))
    hidden = jnp.tanh(context.astype(jnp.float32)).astype(jnp.bfloat16)
    context_drive = jnp.dot(context, context_gate_weight, preferred_element_type=jnp.float32)
    for iteration in range(ITERS):
        rimmed_state = extended(hidden, (("rows", 0), ("tgt", 1)), 1)
        from_flow = (
            motion[0][..., None] * motion_gate_weight[0]
            + motion[1][..., None] * motion_gate_weight[1]
        )
        gate_values = jax.nn.sigmoid(
            kernel_tap_sum(rimmed_state, hidden_gate_weight, band_height, dilated_width, 1)
            + context_drive[..., : 2 * hidden_w]
            + from_flow[..., : 2 * hidden_w]
        )
        update = gate_values[..., :hidden_w]
        reset_gate = gate_values[..., hidden_w:]
        reset_hidden = (reset_gate * hidden.astype(jnp.float32)).astype(jnp.bfloat16)
        candidate = jnp.tanh(
            jnp.dot(reset_hidden, candidate_weight, preferred_element_type=jnp.float32)
            + context_drive[..., 2 * hidden_w :]
            + from_flow[..., 2 * hidden_w :]
        )
        hidden = ((1.0 - update) * hidden.astype(jnp.float32) + update * candidate).astype(
            jnp.bfloat16
        )
        increment = jnp.dot(
            hidden.astype(jnp.float32), motion_head_weight, precision=lax.Precision.HIGHEST
        )
        motion = motion + jnp.moveaxis(increment, -1, 0)
    return (motion, hidden)


def solution(mesh):
    in_specs = (P("rows", "tgt", None), P("rows", None), P(), P(), P(), P(), P(), P(), P())
    out_specs = (P(None, "rows", "tgt"), P("rows", "tgt", None))
    return jax.shard_map(
        on_device, mesh=mesh, in_specs=in_specs, out_specs=out_specs, check_vma=False
    )
```

profile of v0, /device:TPU:25, one launch (start us, length us, event | category | flops | bytes accessed | tf_op | source)
XLA Modules:
  0.0 196.9 jit_solution(3163129594352775587)
XLA Ops:
  3.0 10.1 %collective-permute-start.1 = (bf16[2,2,64,128]{3,2,1,0:T(8,128)(2,1)S(1)}, bf16[2,2,64,128]{3,2,1,0:T(8,128)(2,1)S(1)}, u32[]{:S(2)}, u32[]{:S(2)}) collective-permute-start(bf16[2,2,64,128]{3,2,1,0:T(8,128)(2,1)S(1)} %get-tuple-element.59), channel_id=1, source_target_pairs={{4,0},{8,4},{12,8},{16,12},{20,16},{24,20},{28,24},{32,28},{36,32}... | collective-permute-start | bytes 196616 | tf_op jit(solution)/shard_map/ppermute | solution.py:19
  13.1 1.9 collective-permute-start
  19.8 2.8 %collective-permute-done = bf16[2,2,64,128]{3,2,1,0:T(8,128)(2,1)S(1)} collective-permute-done((bf16[2,2,64,128]{3,2,1,0:T(8,128)(2,1)S(1)}, bf16[2,2,64,128]{3,2,1,0:T(8,128)(2,1)S(1)}, u32[]{:S(2)}, u32[]{:S(2)}) %collective-permute-start) | collective-permute-done | bytes 65568 | tf_op jit(solution)/shard_map/ppermute | solution.py:18
  22.6 4.2 %collective-permute-start.2 = (bf16[2,12,2,128]{3,2,1,0:T(2,128)(2,1)S(1)}, bf16[2,12,2,128]{3,2,1,0:T(2,128)(2,1)S(1)}, u32[]{:S(2)}, u32[]{:S(2)}) collective-permute-start(bf16[2,12,2,128]{3,2,1,0:T(2,128)(2,1)S(1)} %get-tuple-element.54), channel_id=1, source_target_pairs={{0,1},{1,2},{2,3},{4,5},{5,6},{6,7},{8,9},{9,10},{10,11},{12,13},{... | collective-permute-start | bytes 36872 | tf_op jit(solution)/shard_map/ppermute | solution.py:18
  26.8 1.9 collective-permute-start.3
  33.5 6.4 %all-gather = bf16[1,8,256,128]{3,2,1,0:T(8,128)(2,1)S(1)} all-gather(bf16[1,8,64,128]{3,2,1,0:T(8,128)(2,1)S(1)} %get-tuple-element.56), channel_id=2, replica_groups=mesh['rows'=64,'tgt'=4] {'tgt'}, dimensions={2}, use_global_device_ids=true | all-gather | bytes 655360 | tf_op jit(solution)/shard_map/all_gather | solution.py:87
  41.8 7.9 %collective-permute-start.5 = (bf16[8,256,128]{2,1,0:T(8,128)(2,1)S(1)}, bf16[8,256,128]{2,1,0:T(8,128)(2,1)S(1)}, u32[]{:S(2)}, u32[]{:S(2)}) collective-permute-start(bf16[8,256,128]{2,1,0:T(8,128)(2,1)S(1)} %bitcast.235), channel_id=1, source_target_pairs={{4,0},{8,4},{12,8},{16,12},{20,16},{24,20},{28,24},{32,28},{36,32}... | collective-permute-start | bytes 1572872 | tf_op jit(solution)/shard_map/ppermute | solution.py:27
  49.8 1.9 collective-permute-start.7
  51.7 3.4 %collective-permute-start.6 = (bf16[1,64,128]{2,1,0:T(8,128)(2,1)S(1)}, bf16[1,64,128]{2,1,0:T(8,128)(2,1)S(1)}, u32[]{:S(2)}, u32[]{:S(2)}) collective-permute-start(bf16[1,64,128]{2,1,0:T(8,128)(2,1)S(1)} %get-tuple-element.76), channel_id=1, source_target_pairs={{0,4},{4,8},{8,12},{12,16},{16,20},{20,24},{24,28},{28,32},{32,36}... | collective-permute-start | bytes 49160 | tf_op jit(solution)/shard_map/ppermute | solution.py:18
  56.4 4.4 %collective-permute-done.7 = bf16[1,64,128]{2,1,0:T(8,128)(2,1)S(1)} collective-permute-done((bf16[1,64,128]{2,1,0:T(8,128)(2,1)S(1)}, bf16[1,64,128]{2,1,0:T(8,128)(2,1)S(1)}, u32[]{:S(2)}, u32[]{:S(2)}) %collective-permute-start.7) | collective-permute-done | bytes 16416 | tf_op jit(solution)/shard_map/ppermute | solution.py:19
  60.8 4.7 %collective-permute-start.8 = (bf16[10,1,128]{2,1,0:T(2,128)(2,1)S(1)}, bf16[10,1,128]{2,1,0:T(2,128)(2,1)S(1)}, u32[]{:S(2)}, u32[]{:S(2)}) collective-permute-start(bf16[10,1,128]{2,1,0:T(2,128)(2,1)S(1)} %get-tuple-element.70), channel_id=1, source_target_pairs={{0,1},{1,2},{2,3},{4,5},{5,6},{6,7},{8,9},{9,10},{10,11},{12,13},{... | collective-permute-start | bytes 7688 | tf_op jit(solution)/shard_map/ppermute | solution.py:18
  67.8 2.6 %collective-permute-done.9 = bf16[10,1,128]{2,1,0:T(2,128)(2,1)S(1)} collective-permute-done((bf16[10,1,128]{2,1,0:T(2,128)(2,1)S(1)}, bf16[10,1,128]{2,1,0:T(2,128)(2,1)S(1)}, u32[]{:S(2)}, u32[]{:S(2)}) %collective-permute-start.9) | collective-permute-done | bytes 2592 | tf_op jit(solution)/shard_map/ppermute | solution.py:19
  75.9 1.9 add_negate_fusion.1
  78.2 2.3 %exponential_reduce_fusion.2 = (f32[2048]{0:T(1024)}, f32[2048]{0:T(1024)S(1)}, f32[2048]{0:T(1024)S(1)}) fusion(f32[512,2048]{1,0:T(8,128)S(1)} %get-tuple-element.99, f32[2048]{0:T(1024)S(1)} %add_reduce_fusion.2, f32[512]{0:T(512)S(1)} %add_negate_fusion.1, f32[512,2048]{1,0:T(8,128)S(1)} %get-tuple-element.97, f32[512,2048]{1,0:T(8,128)S(1)} %get-tuple-element.95), kind=kLoop, calls=%fused_computation.5 | loop fusion | flops 7333888 | bytes 12617728 | tf_op jit(solution)/shard_map/reduce_sum | solution.py:122
  80.6 2.1 %exponential_reduce_fusion.1 = (f32[2048]{0:T(1024)}, f32[2048]{0:T(1024)}) fusion(f32[512,2048]{1,0:T(8,128)S(1)} %get-tuple-element.97, f32[2048]{0:T(1024)S(1)} %get-tuple-element.48, f32[512]{0:T(512)S(1)} %add_negate_fusion.1, f32[2048]{0:T(1024)S(1)} %get-tuple-element.49, f32[512,2048]{1,0:T(8,128)S(1)} %get-tuple-element.95), kind=kLoop, calls=%fused_computation.4 | loop fusion | flops 6287360 | bytes 8423424 | tf_op jit(solution)/shard_map/reduce_sum | solution.py:122
  83.3 10.9 %pmax.7 = f32[3,2048]{1,0:T(4,128)S(1)} all-reduce(f32[3,2048]{1,0:T(4,128)} %pad_maximum_fusion.6), channel_id=1, replica_groups=mesh['rows'=64,'tgt'=4] {'tgt'}, use_global_device_ids=true, to_apply=%region_9.10 | all-reduce | flops 6144 | bytes 49152 | tf_op jit(solution)/shard_map/pmax | solution.py:125
  95.6 11.5 %psum.7 = f32[3,2048]{1,0:T(4,128)} all-reduce(f32[3,2048]{1,0:T(4,128)} %maximum_multiply_fusion), channel_id=1, replica_groups=mesh['rows'=64,'tgt'=4] {'tgt'}, use_global_device_ids=true, to_apply=%region_13.14 | all-reduce | flops 6144 | bytes 49152 | tf_op jit(solution)/shard_map/psum | solution.py:126
  108.0 7.3 %fusion.1 = f32[512,2]{0,1:T(2,128)S(1)} fusion(f32[512,2048]{1,0:T(8,128)} %copy-done.4, f32[2048]{0:T(1024)S(1)} %bitcast.254, f32[512]{0:T(512)S(1)} %add_negate_fusion.1, pred[]{:T(512)} %bitcast.1, f32[2048,1]{0,1:T(1,128)} %get-tuple-element.102, f32[2048,1]{0,1:T(1,128)} %get-tuple-element.103), kind=kOutput, calls=%fused_computation.16 | convolution fusion | flops 28315648 | bytes 4225025 | tf_op jit(solution)/shard_map/dot_general | solution.py:157
  115.4 6.9 %fusion.4 = (f32[512]{0:T(512)S(1)}, f32[512]{0:T(512)S(1)}, f32[512]{0:T(512)S(1)}) fusion(f32[512,2048]{1,0:T(8,128)} %copy-done.3, f32[2048]{0:T(1024)S(1)} %bitcast.250, f32[512]{0:T(512)S(1)} %add_negate_fusion.1, pred[]{:T(512)} %bitcast.37, f32[2048]{0:T(1024)S(1)} %bitcast.255, f32[512,2048]{1,0:T(8,128)} %copy-done.4, pred[]{:T(512)} %bitcast.1, ...), kind=kLoop, calls=%fused_computation.19 | loop fusion | flops 12581376 | bytes 12615683 | tf_op jit(solution)/shard_map/reduce_sum | solution.py:154
  124.3 7.8 %fusion.84 = f32[512,2]{0,1:T(2,128)} fusion(f32[512,2]{0,1:T(2,128)} %scatter-add.10, f32[512,2048]{1,0:T(8,128)} %copy-done.1, f32[2048]{0:T(1024)S(1)} %bitcast.253, f32[512]{0:T(512)S(1)} %add_negate_fusion.1, pred[]{:T(512)} %bitcast.35, f32[2048,1]{0,1:T(1,128)S(1)} %copy-done.13, f32[2048,1]{0,1:T(1,128)S(1)} %copy-done.14), kind=kOutput, calls=%fused_computation.115 | convolution fusion | flops 28316672 | bytes 4229121 | tf_op jit(solution)/shard_map/dot_general | solution.py:157
  134.1 7.2 %fusion.83 = f32[512,2]{0,1:T(2,128)S(1)} fusion(f32[512,2]{0,1:T(2,128)} %scatter-add.11, f32[512,2048]{1,0:T(8,128)} %copy-done.3, f32[2048]{0:T(1024)S(1)} %bitcast.251, f32[512]{0:T(512)S(1)} %add_negate_fusion.1, pred[]{:T(512)} %bitcast.37, f32[2048,1]{0,1:T(1,128)} %get-tuple-element.102, f32[2048,1]{0,1:T(1,128)} %get-tuple-element.103), kind=kOutput, calls=%fused_computation.114 | convolution fusion | flops 28316672 | bytes 4229121 | tf_op jit(solution)/shard_map/dot_general | solution.py:157
  145.7 8.8 %collective-permute-start.11 = (bf16[1,64,128]{2,1,0:T(8,128)(2,1)S(1)}, bf16[1,64,128]{2,1,0:T(8,128)(2,1)S(1)}, u32[]{:S(2)}, u32[]{:S(2)}) collective-permute-start(bf16[1,64,128]{2,1,0:T(8,128)(2,1)S(1)} %get-tuple-element.75), channel_id=1, source_target_pairs={{4,0},{8,4},{12,8},{16,12},{20,16},{24,20},{28,24},{32,28},{36,32}... | collective-permute-start | bytes 49160 | tf_op jit(solution)/shard_map/ppermute | solution.py:19
  154.6 1.9 collective-permute-start.10
  156.9 6.6 %collective-permute-done.10 = bf16[1,64,128]{2,1,0:T(8,128)(2,1)S(1)} collective-permute-done((bf16[1,64,128]{2,1,0:T(8,128)(2,1)S(1)}, bf16[1,64,128]{2,1,0:T(8,128)(2,1)S(1)}, u32[]{:S(2)}, u32[]{:S(2)}) %collective-permute-start.10) | collective-permute-done | bytes 16416 | tf_op jit(solution)/shard_map/ppermute | solution.py:18
  163.6 4.4 %collective-permute-start.12 = (bf16[10,1,128]{2,1,0:T(2,128)(2,1)S(1)}, bf16[10,1,128]{2,1,0:T(2,128)(2,1)S(1)}, u32[]{:S(2)}, u32[]{:S(2)}) collective-permute-start(bf16[10,1,128]{2,1,0:T(2,128)(2,1)S(1)} %get-tuple-element.66), channel_id=1, source_target_pairs={{0,1},{1,2},{2,3},{4,5},{5,6},{6,7},{8,9},{9,10},{10,11},{12,13},{... | collective-permute-start | bytes 7688 | tf_op jit(solution)/shard_map/ppermute | solution.py:18
  168.0 1.9 collective-permute-start.13
  170.3 2.6 %collective-permute-done.13 = bf16[10,1,128]{2,1,0:T(2,128)(2,1)S(1)} collective-permute-done((bf16[10,1,128]{2,1,0:T(2,128)(2,1)S(1)}, bf16[10,1,128]{2,1,0:T(2,128)(2,1)S(1)}, u32[]{:S(2)}, u32[]{:S(2)}) %collective-permute-start.13) | collective-permute-done | bytes 2592 | tf_op jit(solution)/shard_map/ppermute | solution.py:19
  175.1 2.0 collective-permute-start.15
  177.1 3.3 %collective-permute-start.14 = (bf16[1,64,128]{2,1,0:T(8,128)(2,1)S(1)}, bf16[1,64,128]{2,1,0:T(8,128)(2,1)S(1)}, u32[]{:S(2)}, u32[]{:S(2)}) collective-permute-start(bf16[1,64,128]{2,1,0:T(8,128)(2,1)S(1)} %get-tuple-element.72), channel_id=1, source_target_pairs={{0,4},{4,8},{8,12},{12,16},{16,20},{20,24},{24,28},{28,32},{32,36}... | collective-permute-start | bytes 49160 | tf_op jit(solution)/shard_map/ppermute | solution.py:18
  180.8 5.2 %collective-permute-done.14 = bf16[1,64,128]{2,1,0:T(8,128)(2,1)S(1)} collective-permute-done((bf16[1,64,128]{2,1,0:T(8,128)(2,1)S(1)}, bf16[1,64,128]{2,1,0:T(8,128)(2,1)S(1)}, u32[]{:S(2)}, u32[]{:S(2)}) %collective-permute-start.14) | collective-permute-done | bytes 16416 | tf_op jit(solution)/shard_map/ppermute | solution.py:18
  186.1 3.1 %collective-permute-start.16 = (bf16[10,1,128]{2,1,0:T(2,128)(2,1)S(1)}, bf16[10,1,128]{2,1,0:T(2,128)(2,1)S(1)}, u32[]{:S(2)}, u32[]{:S(2)}) collective-permute-start(bf16[10,1,128]{2,1,0:T(2,128)(2,1)S(1)} %get-tuple-element.62), channel_id=1, source_target_pairs={{0,1},{1,2},{2,3},{4,5},{5,6},{6,7},{8,9},{9,10},{10,11},{12,13},{... | collective-permute-start | bytes 7688 | tf_op jit(solution)/shard_map/ppermute | solution.py:18
  191.5 2.6 %collective-permute-done.17 = bf16[10,1,128]{2,1,0:T(2,128)(2,1)S(1)} collective-permute-done((bf16[10,1,128]{2,1,0:T(2,128)(2,1)S(1)}, bf16[10,1,128]{2,1,0:T(2,128)(2,1)S(1)}, u32[]{:S(2)}, u32[]{:S(2)}) %collective-permute-start.17) | collective-permute-done | bytes 2592 | tf_op jit(solution)/shard_map/ppermute | solution.py:19
  (137 shorter events, 42.9 us)
Async XLA Ops:
  0.6 54.5 %copy-start = (bf16[128,384]{1,0:T(8,128)(2,1)S(1)}, bf16[128,384]{1,0:T(8,128)(2,1)}, u32[]{:S(2)}) copy-start(bf16[128,384]{1,0:T(8,128)(2,1)} %param.19) | copy-start | bytes 294916
  0.6 31.4 %copy-start.7 = (bf16[9,128,128]{2,1,0:T(8,128)(2,1)S(1)}, bf16[9,128,128]{2,1,0:T(8,128)(2,1)}, u32[]{:S(2)}) copy-start(bf16[9,128,128]{2,1,0:T(8,128)(2,1)} %param.18) | copy-start | bytes 884740
  3.0 16.9 %collective-permute-start.1 = (bf16[2,2,64,128]{3,2,1,0:T(8,128)(2,1)S(1)}, bf16[2,2,64,128]{3,2,1,0:T(8,128)(2,1)S(1)}, u32[]{:S(2)}, u32[]{:S(2)}) collective-permute-start(bf16[2,2,64,128]{3,2,1,0:T(8,128)(2,1)S(1)} %get-tuple-element.59), channel_id=1, source_target_pairs={{4,0},{8,4},{12,8},{16,12},{20,16},{24,20},{28,24},{32,28},{36,32}... | collective-permute-start | bytes 196616 | tf_op jit(solution)/shard_map/ppermute | solution.py:19
  13.1 9.5 %collective-permute-start = (bf16[2,2,64,128]{3,2,1,0:T(8,128)(2,1)S(1)}, bf16[2,2,64,128]{3,2,1,0:T(8,128)(2,1)S(1)}, u32[]{:S(2)}, u32[]{:S(2)}) collective-permute-start(bf16[2,2,64,128]{3,2,1,0:T(8,128)(2,1)S(1)} %get-tuple-element.58), channel_id=1, source_target_pairs={{0,4},{4,8},{8,12},{12,16},{16,20},{20,24},{24,28},{28,32},{32,36}... | collective-permute-start | bytes 196616 | tf_op jit(solution)/shard_map/ppermute | solution.py:18
  22.6 8.1 %collective-permute-start.2 = (bf16[2,12,2,128]{3,2,1,0:T(2,128)(2,1)S(1)}, bf16[2,12,2,128]{3,2,1,0:T(2,128)(2,1)S(1)}, u32[]{:S(2)}, u32[]{:S(2)}) collective-permute-start(bf16[2,12,2,128]{3,2,1,0:T(2,128)(2,1)S(1)} %get-tuple-element.54), channel_id=1, source_target_pairs={{0,1},{1,2},{2,3},{4,5},{5,6},{6,7},{8,9},{9,10},{10,11},{12,13},{... | collective-permute-start | bytes 36872 | tf_op jit(solution)/shard_map/ppermute | solution.py:18
  26.8 5.0 %collective-permute-start.3 = (bf16[2,12,2,128]{3,2,1,0:T(2,128)(2,1)S(1)}, bf16[2,12,2,128]{3,2,1,0:T(2,128)(2,1)S(1)}, u32[]{:S(2)}, u32[]{:S(2)}) collective-permute-start(bf16[2,12,2,128]{3,2,1,0:T(2,128)(2,1)S(1)} %get-tuple-element.55), channel_id=1, source_target_pairs={{1,0},{2,1},{3,2},{5,4},{6,5},{7,6},{9,8},{10,9},{11,10},{13,12},{... | collective-permute-start | bytes 36872 | tf_op jit(solution)/shard_map/ppermute | solution.py:19
  33.5 22.6 %copy-start.5 = (bf16[9,128,256]{2,1,0:T(8,128)(2,1)S(1)}, bf16[9,128,256]{2,1,0:T(8,128)(2,1)}, u32[]{:S(2)}) copy-start(bf16[9,128,256]{2,1,0:T(8,128)(2,1)} %param.20) | copy-start | bytes 1769476
  39.9 32.4 %collective-permute-start.4 = (bf16[8,256,128]{2,1,0:T(8,128)(2,1)S(1)}, bf16[8,256,128]{2,1,0:T(8,128)(2,1)S(1)}, u32[]{:S(2)}, u32[]{:S(2)}) collective-permute-start(bf16[8,256,128]{2,1,0:T(8,128)(2,1)S(1)} %bitcast.234), channel_id=1, source_target_pairs={{0,4},{4,8},{8,12},{12,16},{16,20},{20,24},{24,28},{28,32},{32,36}... | collective-permute-start | bytes 1572872 | tf_op jit(solution)/shard_map/ppermute | solution.py:27
  41.8 31.3 %collective-permute-start.5 = (bf16[8,256,128]{2,1,0:T(8,128)(2,1)S(1)}, bf16[8,256,128]{2,1,0:T(8,128)(2,1)S(1)}, u32[]{:S(2)}, u32[]{:S(2)}) collective-permute-start(bf16[8,256,128]{2,1,0:T(8,128)(2,1)S(1)} %bitcast.235), channel_id=1, source_target_pairs={{4,0},{8,4},{12,8},{16,12},{20,16},{24,20},{28,24},{32,28},{36,32}... | collective-permute-start | bytes 1572872 | tf_op jit(solution)/shard_map/ppermute | solution.py:27
  49.8 11.0 %collective-permute-start.7 = (bf16[1,64,128]{2,1,0:T(8,128)(2,1)S(1)}, bf16[1,64,128]{2,1,0:T(8,128)(2,1)S(1)}, u32[]{:S(2)}, u32[]{:S(2)}) collective-permute-start(bf16[1,64,128]{2,1,0:T(8,128)(2,1)S(1)} %get-tuple-element.77), channel_id=1, source_target_pairs={{4,0},{8,4},{12,8},{16,12},{20,16},{24,20},{28,24},{32,28},{36,32}... | collective-permute-start | bytes 49160 | tf_op jit(solution)/shard_map/ppermute | solution.py:19
  51.7 9.0 %collective-permute-start.6 = (bf16[1,64,128]{2,1,0:T(8,128)(2,1)S(1)}, bf16[1,64,128]{2,1,0:T(8,128)(2,1)S(1)}, u32[]{:S(2)}, u32[]{:S(2)}) collective-permute-start(bf16[1,64,128]{2,1,0:T(8,128)(2,1)S(1)} %get-tuple-element.76), channel_id=1, source_target_pairs={{0,4},{4,8},{8,12},{12,16},{16,20},{20,24},{24,28},{28,32},{32,36}... | collective-permute-start | bytes 49160 | tf_op jit(solution)/shard_map/ppermute | solution.py:18
  56.1 24.4 %copy-start.1 = (f32[512,2048]{1,0:T(8,128)}, f32[512,2048]{1,0:T(8,128)S(1)}, u32[]{:S(2)}) copy-start(f32[512,2048]{1,0:T(8,128)S(1)} %get-tuple-element.97) | copy-start | bytes 12582916
  60.8 7.0 %collective-permute-start.8 = (bf16[10,1,128]{2,1,0:T(2,128)(2,1)S(1)}, bf16[10,1,128]{2,1,0:T(2,128)(2,1)S(1)}, u32[]{:S(2)}, u32[]{:S(2)}) collective-permute-start(bf16[10,1,128]{2,1,0:T(2,128)(2,1)S(1)} %get-tuple-element.70), channel_id=1, source_target_pairs={{0,1},{1,2},{2,3},{4,5},{5,6},{6,7},{8,9},{9,10},{10,11},{12,13},{... | collective-permute-start | bytes 7688 | tf_op jit(solution)/shard_map/ppermute | solution.py:18
  65.4 4.9 %collective-permute-start.9 = (bf16[10,1,128]{2,1,0:T(2,128)(2,1)S(1)}, bf16[10,1,128]{2,1,0:T(2,128)(2,1)S(1)}, u32[]{:S(2)}, u32[]{:S(2)}) collective-permute-start(bf16[10,1,128]{2,1,0:T(2,128)(2,1)S(1)} %get-tuple-element.71), channel_id=1, source_target_pairs={{1,0},{2,1},{3,2},{5,4},{6,5},{7,6},{9,8},{10,9},{11,10},{13,12},{... | collective-permute-start | bytes 7688 | tf_op jit(solution)/shard_map/ppermute | solution.py:19
  73.2 5.1 %copy-start.4 = (f32[512,2048]{1,0:T(8,128)}, f32[512,2048]{1,0:T(8,128)S(1)}, u32[]{:S(2)}) copy-start(f32[512,2048]{1,0:T(8,128)S(1)} %get-tuple-element.99) | copy-start | bytes 12582916
  74.0 6.6 %copy-start.3 = (f32[512,2048]{1,0:T(8,128)}, f32[512,2048]{1,0:T(8,128)S(1)}, u32[]{:S(2)}) copy-start(f32[512,2048]{1,0:T(8,128)S(1)} %get-tuple-element.95) | copy-start | bytes 12582916
  107.1 8.3 %copy-start.2 = (f32[512,2048]{1,0:T(8,128)S(1)}, f32[512,2048]{1,0:T(8,128)}, u32[]{:S(2)}) copy-start(f32[512,2048]{1,0:T(8,128)} %copy-done.1) | copy-start | bytes 12582916
  115.4 7.6 %copy-start.15 = (f32[512,2]{0,1:T(2,128)}, f32[512,2]{0,1:T(2,128)S(1)}, u32[]{:S(2)}) copy-start(f32[512,2]{0,1:T(2,128)S(1)} %fusion.1) | copy-start | bytes 12292
  115.4 8.9 %copy-start.13 = (f32[2048,1]{0,1:T(1,128)S(1)}, f32[2048,1]{0,1:T(1,128)}, u32[]{:S(2)}) copy-start(f32[2048,1]{0,1:T(1,128)} %get-tuple-element.102) | copy-start | bytes 24580
  115.4 8.9 %copy-start.14 = (f32[2048,1]{0,1:T(1,128)S(1)}, f32[2048,1]{0,1:T(1,128)}, u32[]{:S(2)}) copy-start(f32[2048,1]{0,1:T(1,128)} %get-tuple-element.103) | copy-start | bytes 24580
  124.3 19.1 %copy-start.9 = (f32[384]{0:T(512)S(1)}, f32[384]{0:T(512)}, u32[]{:S(2)}) copy-start(f32[384]{0:T(512)} %get-tuple-element.42) | copy-start | bytes 4612
  124.3 19.1 %copy-start.10 = (f32[384]{0:T(512)S(1)}, f32[384]{0:T(512)}, u32[]{:S(2)}) copy-start(f32[384]{0:T(512)} %get-tuple-element.43) | copy-start | bytes 4612
  134.1 10.9 %copy-start.8 = (bf16[128,128]{1,0:T(8,128)(2,1)S(1)}, bf16[128,128]{1,0:T(8,128)(2,1)}, u32[]{:S(2)}) copy-start(bf16[128,128]{1,0:T(8,128)(2,1)} %param.21) | copy-start | bytes 98308
  141.3 3.9 %copy-start.11 = (f32[128,2]{0,1:T(2,128)S(1)}, f32[128,2]{0,1:T(2,128)}, u32[]{:S(2)}) copy-start(f32[128,2]{0,1:T(2,128)} %param.23) | copy-start | bytes 3076
  145.7 11.2 %collective-permute-start.11 = (bf16[1,64,128]{2,1,0:T(8,128)(2,1)S(1)}, bf16[1,64,128]{2,1,0:T(8,128)(2,1)S(1)}, u32[]{:S(2)}, u32[]{:S(2)}) collective-permute-start(bf16[1,64,128]{2,1,0:T(8,128)(2,1)S(1)} %get-tuple-element.75), channel_id=1, source_target_pairs={{4,0},{8,4},{12,8},{16,12},{20,16},{24,20},{28,24},{32,28},{36,32}... | collective-permute-start | bytes 49160 | tf_op jit(solution)/shard_map/ppermute | solution.py:19
  154.6 9.0 %collective-permute-start.10 = (bf16[1,64,128]{2,1,0:T(8,128)(2,1)S(1)}, bf16[1,64,128]{2,1,0:T(8,128)(2,1)S(1)}, u32[]{:S(2)}, u32[]{:S(2)}) collective-permute-start(bf16[1,64,128]{2,1,0:T(8,128)(2,1)S(1)} %get-tuple-element.74), channel_id=1, source_target_pairs={{0,4},{4,8},{8,12},{12,16},{16,20},{20,24},{24,28},{28,32},{32,36}... | collective-permute-start | bytes 49160 | tf_op jit(solution)/shard_map/ppermute | solution.py:18
  163.6 6.7 %collective-permute-start.12 = (bf16[10,1,128]{2,1,0:T(2,128)(2,1)S(1)}, bf16[10,1,128]{2,1,0:T(2,128)(2,1)S(1)}, u32[]{:S(2)}, u32[]{:S(2)}) collective-permute-start(bf16[10,1,128]{2,1,0:T(2,128)(2,1)S(1)} %get-tuple-element.66), channel_id=1, source_target_pairs={{0,1},{1,2},{2,3},{4,5},{5,6},{6,7},{8,9},{9,10},{10,11},{12,13},{... | collective-permute-start | bytes 7688 | tf_op jit(solution)/shard_map/ppermute | solution.py:18
  168.0 4.9 %collective-permute-start.13 = (bf16[10,1,128]{2,1,0:T(2,128)(2,1)S(1)}, bf16[10,1,128]{2,1,0:T(2,128)(2,1)S(1)}, u32[]{:S(2)}, u32[]{:S(2)}) collective-permute-start(bf16[10,1,128]{2,1,0:T(2,128)(2,1)S(1)} %get-tuple-element.67), channel_id=1, source_target_pairs={{1,0},{2,1},{3,2},{5,4},{6,5},{7,6},{9,8},{10,9},{11,10},{13,12},{... | collective-permute-start | bytes 7688 | tf_op jit(solution)/shard_map/ppermute | solution.py:19
  175.1 5.7 %collective-permute-start.15 = (bf16[1,64,128]{2,1,0:T(8,128)(2,1)S(1)}, bf16[1,64,128]{2,1,0:T(8,128)(2,1)S(1)}, u32[]{:S(2)}, u32[]{:S(2)}) collective-permute-start(bf16[1,64,128]{2,1,0:T(8,128)(2,1)S(1)} %get-tuple-element.73), channel_id=1, source_target_pairs={{4,0},{8,4},{12,8},{16,12},{20,16},{24,20},{28,24},{32,28},{36,32}... | collective-permute-start | bytes 49160 | tf_op jit(solution)/shard_map/ppermute | solution.py:19
  177.1 9.0 %collective-permute-start.14 = (bf16[1,64,128]{2,1,0:T(8,128)(2,1)S(1)}, bf16[1,64,128]{2,1,0:T(8,128)(2,1)S(1)}, u32[]{:S(2)}, u32[]{:S(2)}) collective-permute-start(bf16[1,64,128]{2,1,0:T(8,128)(2,1)S(1)} %get-tuple-element.72), channel_id=1, source_target_pairs={{0,4},{4,8},{8,12},{12,16},{16,20},{20,24},{24,28},{28,32},{32,36}... | collective-permute-start | bytes 49160 | tf_op jit(solution)/shard_map/ppermute | solution.py:18
  186.1 5.4 %collective-permute-start.16 = (bf16[10,1,128]{2,1,0:T(2,128)(2,1)S(1)}, bf16[10,1,128]{2,1,0:T(2,128)(2,1)S(1)}, u32[]{:S(2)}, u32[]{:S(2)}) collective-permute-start(bf16[10,1,128]{2,1,0:T(2,128)(2,1)S(1)} %get-tuple-element.62), channel_id=1, source_target_pairs={{0,1},{1,2},{2,3},{4,5},{5,6},{6,7},{8,9},{9,10},{10,11},{12,13},{... | collective-permute-start | bytes 7688 | tf_op jit(solution)/shard_map/ppermute | solution.py:18
  189.1 4.9 %collective-permute-start.17 = (bf16[10,1,128]{2,1,0:T(2,128)(2,1)S(1)}, bf16[10,1,128]{2,1,0:T(2,128)(2,1)S(1)}, u32[]{:S(2)}, u32[]{:S(2)}) collective-permute-start(bf16[10,1,128]{2,1,0:T(2,128)(2,1)S(1)} %get-tuple-element.63), channel_id=1, source_target_pairs={{1,0},{2,1},{3,2},{5,4},{6,5},{7,6},{9,8},{10,9},{11,10},{13,12},{... | collective-permute-start | bytes 7688 | tf_op jit(solution)/shard_map/ppermute | solution.py:19
  (2 other events, 1.6 us)
where the time goes:
time: 198 us; the launch traced here: 197 us
  starting transfers between devices  67.2 us (34%)
  matrix products  41.2 us (21%)
  blocking collectives  28.7 us (14%)
  waiting for transfers between devices  27.9 us (14%)
  other arithmetic  24.3 us (12%)
  local copies, waits for them, and re-layouts  6.11 us (3%)
    ppermute x8, starting transfers between devices, extended(): after = lax.ppermute(initial, axis, down)  30.5 us
    ppermute x8, starting transfers between devices, extended(): before = lax.ppermute(last, axis, up)  26.8 us
    dot_general x3, matrix products, on_device(): moment = moment + jnp.dot(coupling, coords, precision=lax.Precision.HIGHEST)  22.4 us
    ppermute x8, waiting for transfers between devices, extended(): before = lax.ppermute(last, axis, up)  14.7 us
    ppermute x8, waiting for transfers between devices, extended(): after = lax.ppermute(initial, axis, down)  13.2 us
    dot_general x36, matrix products, kernel_tap_sum(): jnp.dot(tap_piece, weights[3 * row_tap + col_tap], preferred_element_type...  12.2 us
    psum x1, blocking collectives, on_device(): sum_all = lax.psum(col_sum * jnp.exp(col_peak - top_all), 'tgt')  11.5 us
    pmax x1, blocking collectives, on_device(): top_all = lax.pmax(col_peak, 'tgt')  10.9 us
  transfers between devices with their start and end apart: 18, of which 8 were waited for; matrix products, arithmetic and copies ran while one was open for 7% of the time, Pallas kernels for 0%

commit v1 on v0

v1 whole, which is shorter than its diff:
```python
import functools
import math

import jax
import jax.numpy as jnp
from jax import lax
from jax.experimental import pallas as pl
from jax.experimental.pallas import tpu as pltpu
from jax.sharding import PartitionSpec as P

BF = jnp.bfloat16
F32 = jnp.float32
LOG2E = 1.4426950408889634
BAND = 8
COLS = 64
WIDE = 256
CH = 128
PADW = 96
MINUS, PLUS = -1, 1


def roll0(x, shift):
    return pltpu.roll(x, shift % x.shape[0], axis=0)


def dot(a, b):
    return jnp.dot(a, b, preferred_element_type=F32)


def dot_nt(a, b):
    return lax.dot_general(a, b, (((1,), (1,)), ((), ())), preferred_element_type=F32)


def placement(rows, halo, side):
    token = lax.broadcasted_iota(jnp.int32, (rows * 16, 48), 0)
    strip = lax.broadcasted_iota(jnp.int32, (rows * 16, 48), 1)
    row, col = token >> 4, token & 15
    base = 2 * (row + 8 - halo)
    if side == 0:
        hit = (col >= 14) & (strip == base + col - 14)
    else:
        hit = (col < 2) & (strip == base + col)
    return jnp.where(hit, 1.0, 0.0).astype(BF)


def strip_pick():
    strip = lax.broadcasted_iota(jnp.int32, (32, BAND * COLS), 0)
    token = lax.broadcasted_iota(jnp.int32, (32, BAND * COLS), 1)
    row, col = (strip & 15) >> 1, strip & 1
    wanted = row * COLS + col + jnp.where(strip >= 16, COLS - 2, 0)
    return jnp.where(token == wanted, 1.0, 0.0).astype(BF)


def kernel(
    n_rows,
    frames,
    window,
    patch_w,
    dil_w,
    ctx_w,
    gate_w,
    cand_w,
    mgate_w,
    mhead_w,
    motion_out,
    hidden_out,
    raw,
    e1,
    f1,
    sb,
    qb,
    rp,
    e0,
    hp,
    sbuf,
    sx,
    st,
    sr,
    gs,
    rowmax,
    rowsum,
    f0,
    drive,
    wc,
    wh,
    hw,
    acc,
    raw_send,
    raw_recv,
    fwd_send,
    fwd_recv,
    halo_send,
    halo_recv,
    col_send,
    col_recv,
):
    r = lax.axis_index("rows")
    t = lax.axis_index("tgt")
    sib = t + 1 - 2 * (t % 2)
    far = (t + 2) % 4
    far_sib = 3 - t

    def row_ok(d):
        return (r + d >= 0) & (r + d < n_rows)

    def col_ok(d):
        return (t + d >= 0) & (t + d < 4)

    def remote(src, dst, send, recv, rr, tt):
        return pltpu.make_async_remote_copy(
            src_ref=src,
            dst_ref=dst,
            send_sem=send,
            recv_sem=recv,
            device_id=(rr, tt),
            device_id_type=pl.DeviceIdType.MESH,
        )

    def zero(ref):
        ref[...] = jnp.zeros(ref.shape, ref.dtype)

    for b in (t, far):
        for d, lo, hi in ((-1, 2, 10), (-2, 0, 2), (1, 18, 26), (2, 26, 28)):

            @pl.when(jnp.logical_not(row_ok(d)))
            def _():
                zero(raw.at[b, lo:hi])

    for d, rp_lo, rp_hi, hp_row, slot in ((-1, 0, 2, 0, 0), (1, 10, 12, 9, 2)):

        @pl.when(jnp.logical_not(row_ok(d)))
        def _():
            rp[rp_lo:rp_hi, 16:80] = jnp.zeros((2, COLS, CH), BF)
            for e in range(3):
                hp[e, hp_row, 16:80] = jnp.zeros((COLS, CH), BF)
            for e in range(4):
                for side in range(2):
                    zero(sx.at[e, side, slot])

    for d, side in ((-1, 0), (1, 1)):

        @pl.when(jnp.logical_not(col_ok(d)))
        def _():
            for e in range(4):
                for slot in range(3):
                    zero(sx.at[e, side, slot])

    barrier = pltpu.get_barrier_semaphore()
    count = 3

    def greet(rr, tt):
        pl.semaphore_signal(
            barrier, inc=1, device_id=(rr, tt), device_id_type=pl.DeviceIdType.MESH
        )

    for tt in (far, sib, far_sib):
        greet(r, tt)
    for d in (1, -1, 2, -2):
        partners = (t, far) if abs(d) == 2 else (t, far, sib, far_sib)

        @pl.when(row_ok(d))
        def _():
            for tt in partners:
                greet(r + d, tt)

        count = count + len(partners) * row_ok(d).astype(jnp.int32)

    whole = frames[...].astype(F32)
    half0 = whole[:, 0:32].reshape(BAND * 32, CH)
    half1 = whole[:, 32:64].reshape(BAND * 32, CH)
    lane = lax.broadcasted_iota(jnp.int32, (BAND * 32, CH), 1)
    packed = jnp.where(lane < 64, pltpu.roll(half0, 64, axis=1), half1)
    raw[t, 10:18] = packed.astype(BF).reshape(BAND, 32, CH)
    pick = strip_pick()
    sbuf[0] = dot(pick, frames[...].reshape(BAND * COLS, CH)).astype(BF).reshape(2, 16, CH)

    pl.semaphore_wait(barrier, count)

    spans = {0: ((10, 18), (10, 18)), 1: ((10, 18), (2, 10)), -1: ((10, 18), (18, 26)),
             2: ((16, 18), (0, 2)), -2: ((10, 12), (26, 28))}

    def raw_copy(w, d, block):
        (s_lo, s_hi), (d_lo, d_hi) = spans[d]
        return remote(
            raw.at[block, s_lo:s_hi],
            raw.at[block, d_lo:d_hi],
            raw_send.at[w, d + 2],
            raw_recv.at[w, d + 2],
            r + d,
            far if w else t,
        )

    def halo_copies(e):
        copies = []
        for d, slot in ((1, 0), (-1, 2)):
            if e == 0:
                src = frames.at[6:8] if d == 1 else frames.at[0:2]
                dst = rp.at[0:2, 16:80] if d == 1 else rp.at[10:12, 16:80]
            else:
                src = hp.at[e - 1, 8, 16:80] if d == 1 else hp.at[e - 1, 1, 16:80]
                dst = hp.at[e - 1, 0, 16:80] if d == 1 else hp.at[e - 1, 9, 16:80]
            copies.append((d, 0, src, dst))
        for dt in (-1, 1):
            own = 0 if dt == -1 else 1
            for d in (0, 1, -1):
                copies.append((d, dt, sbuf.at[e, own], sx.at[e, 1 - own, 1 - d]))
        return [
            (d, dt, remote(src, dst, halo_send.at[e, k], halo_recv.at[e, k], r + d, t + dt))
            for k, (d, dt, src, dst) in enumerate(copies)
        ]

    def start_halo(e):
        for d, dt, copy in halo_copies(e):

            @pl.when(row_ok(d) & col_ok(dt))
            def _():
                copy.start()

    def wait_halo(e):
        for d, dt, copy in halo_copies(e):

            @pl.when(row_ok(-d) & col_ok(-dt))
            def _():
                copy.wait_recv()

    def end_halo(e):
        for d, dt, copy in halo_copies(e):

            @pl.when(row_ok(d) & col_ok(dt))
            def _():
                copy.wait_send()

    def fwd_copy(w, chunk, block):
        lo, hi = ((10, 18), (0, 10), (18, 28))[chunk]
        return remote(
            raw.at[block, lo:hi],
            raw.at[block, lo:hi],
            fwd_send.at[w, chunk],
            fwd_recv.at[w, chunk],
            r,
            sib,
        )

    raw_copy(1, 0, t).start()
    for d in (1, -1):
        for w in (1, 0):

            @pl.when(row_ok(d))
            def _():
                raw_copy(w, d, t).start()

    for d in (2, -2):
        for w in (1, 0):

            @pl.when(row_ok(d))
            def _():
                raw_copy(w, d, t).start()

    fwd_copy(0, 0, t).start()
    start_halo(0)

    for a in range(3):
        for b in range(3):
            wc[a * CH : (a + 1) * CH, b * CH : (b + 1) * CH] = dil_w[3 * a + b]
            wh[a * CH : (a + 1) * CH, 2 * b * CH : 2 * (b + 1) * CH] = gate_w[3 * a + b]
    for k in range(2):
        column = jnp.broadcast_to(mhead_w[:, k : k + 1], (CH, CH))
        for part in range(3):
            rounded = column.astype(BF)
            hw[part * CH : (part + 1) * CH, k * CH : (k + 1) * CH] = rounded
            column = column - rounded.astype(F32)
    embed_one = jnp.concatenate([patch_w[...], jnp.zeros((64, CH), BF)], axis=0)
    embed_two = jnp.concatenate(
        [embed_one, jnp.concatenate([jnp.zeros((64, CH), BF), patch_w[...]], axis=0)], axis=1
    )
    rp[2:10, 16:80] = frames[...]

    def forward(w, chunk, arrivals, block):
        for d in arrivals:
            if w == 0 and d == 0:
                continue

            @pl.when(row_ok(-d))
            def _():
                raw_copy(w, d, block).wait_recv()

        if not (w == 0 and chunk == 0):
            fwd_copy(w, chunk, block).start()

    forward(0, 1, (1, 2), t)
    forward(0, 2, (-1, -2), t)
    forward(1, 0, (0,), far)
    forward(1, 1, (1, 2), far)
    forward(1, 2, (-1, -2), far)

    def embed_block(b):
        pair = dot(raw[b].reshape(28 * 32, CH), embed_two).astype(BF)
        start = pl.multiple_of(b * COLS, 32)
        e1[:, pl.ds(start, 32)] = pair[:, :CH].reshape(28, 32, CH)
        later = pl.multiple_of(b * COLS + 32, 32)
        e1[:, pl.ds(later, 32)] = pair[:, CH:].reshape(28, 32, CH)

    embed_block(t)
    embed_block(far)

    wait_halo(0)
    rp[:, 0:16] = dot(placement(12, 2, 0), sx[0, 0].reshape(48, CH)).astype(BF).reshape(12, 16, CH)
    rp[:, 80:96] = dot(placement(12, 2, 1), sx[0, 1].reshape(48, CH)).astype(BF).reshape(12, 16, CH)
    e0[...] = dot(rp[...].reshape(12 * PADW, CH), embed_one).astype(BF).reshape(12, PADW, CH)
    taps = jnp.concatenate([e0[0:8], e0[2:10], e0[4:12]], axis=2).reshape(BAND * PADW, 3 * CH)
    y = dot(taps, wc[...])
    conv = roll0(y[:, :CH], 2) + y[:, CH : 2 * CH] + roll0(y[:, 2 * CH :], -2)
    conv = conv.reshape(BAND, PADW, CH)[:, 16:80].reshape(BAND * COLS, CH)
    own = e0[2:10, 16:80].reshape(BAND * COLS, CH).astype(F32)
    features = (own + jnp.maximum(conv, 0.0)).astype(BF)
    f0[...] = features
    drive[...] = dot(features, ctx_w[...])

    def share(e, state):
        hp[e - 1, 1:9, 16:80] = state.reshape(BAND, COLS, CH)
        sbuf[e] = dot(pick, state).astype(BF).reshape(2, 16, CH)
        start_halo(e)

    share(1, jnp.tanh(features.astype(F32)).astype(BF))

    for w, chunk in ((0, 0), (0, 1), (0, 2), (1, 0), (1, 1), (1, 2)):
        fwd_copy(w, chunk, far_sib if w else sib).wait_recv()
    embed_block(sib)
    embed_block(far_sib)

    column = lax.broadcasted_iota(jnp.int32, (4 * WIDE, CH), 0) & (WIDE - 1)

    def conv_rows(i, carry):
        y0 = i * 4
        taps = jnp.concatenate(
            [e1[pl.ds(y0, 4)], e1[pl.ds(y0 + 2, 4)], e1[pl.ds(y0 + 4, 4)]], axis=2
        ).reshape(4 * WIDE, 3 * CH)
        y = dot(taps, wc[...])
        before = jnp.where(column < 2, 0.0, roll0(y[:, :CH], 2))
        after = jnp.where(column >= WIDE - 2, 0.0, roll0(y[:, 2 * CH :], -2))
        conv = before + y[:, CH : 2 * CH] + after
        own = e1[pl.ds(y0 + 2, 4)].reshape(4 * WIDE, CH).astype(F32)
        f1[pl.ds(y0, 4)] = (own + jnp.maximum(conv, 0.0)).astype(BF).reshape(4, WIDE, CH)
        return carry

    lax.fori_loop(0, 6, conv_rows, 0)

    scale = LOG2E / math.sqrt(CH)
    rowmax[...] = jnp.full(rowmax.shape, -jnp.inf, F32)
    rowsum[...] = jnp.zeros(rowsum.shape, F32)

    def score_row(j, o):
        s = dot_nt(f0[...], f1[j]) * scale
        sb[j] = s
        rowmax[o] = jnp.maximum(rowmax[o], jnp.maximum(s[:, :CH], s[:, CH:]))
        return o

    for o in range(3):
        lax.fori_loop(8 * o, 8 * o + 8, lambda j, c, o=o: (score_row(j, o), c)[1], 0)

    allowed = []
    for o in range(3):
        ok = (window[0, o] == 1) & row_ok(o - 1)
        allowed.append(ok.astype(jnp.int32))
    tokens = BAND * COLS

    def picked(o, x, other):
        return jnp.where(jnp.full(x.shape, allowed[o]) == 1, x, other)

    top = None
    for o in range(3):
        peak = jnp.max(rowmax[o], axis=1, keepdims=True)
        peak = picked(o, jnp.broadcast_to(peak, (tokens, CH)), -jnp.inf)
        top = peak if top is None else jnp.maximum(top, peak)
    rowmax[0] = top

    def mass_row(j, o):
        peak = rowmax[0]
        s = sb[j]
        rowsum[o] += jnp.exp2(s[:, :CH] - peak) + jnp.exp2(s[:, CH:] - peak)

    for o in range(3):
        lax.fori_loop(8 * o, 8 * o + 8, lambda j, c, o=o: (mass_row(j, o), c)[1], 0)
    total = None
    for o in range(3):
        part = picked(o, rowsum[o], 0.0)
        total = part if total is None else total + part
    total = jnp.broadcast_to(jnp.sum(total, axis=1, keepdims=True), (tokens, CH))
    rowmax[1] = -(rowmax[0] + jnp.log(total) * LOG2E)

    def col_row(j, carry):
        pot = rowmax[1]
        shifted = sb[j] + jnp.concatenate([pot, pot], axis=1)
        peak = jnp.max(shifted, axis=0, keepdims=True)
        q = jnp.exp2(shifted - peak)
        qb[j] = q.astype(BF)
        st[0, pl.ds(j, 1), :] = peak
        st[1, pl.ds(j, 1), :] = jnp.sum(q, axis=0, keepdims=True)
        return carry

    lax.fori_loop(0, 24, col_row, 0)

    col_copies = [
        remote(st, sr.at[k], col_send.at[k], col_recv.at[k], r, peer)
        for k, peer in enumerate((sib, far, far_sib))
    ]
    for copy in col_copies:
        copy.start()
    for copy in col_copies:
        copy.wait_recv()
    peak = jnp.maximum(jnp.maximum(st[0], sr[0, 0]), jnp.maximum(sr[1, 0], sr[2, 0]))
    mine = jnp.exp2(st[0] - peak)
    total = st[1] * mine
    for k in range(3):
        total = total + sr[k, 1] * jnp.exp2(sr[k, 0] - peak)
    factor = mine / total
    for o in range(3):
        gs[8 * o : 8 * o + 8] = picked(o, factor[8 * o : 8 * o + 8], 0.0)

    acc[...] = jnp.zeros(acc.shape, F32)
    sub = lax.broadcasted_iota(jnp.int32, (16, WIDE), 0)
    cell_col = lax.broadcasted_iota(jnp.int32, (16, WIDE), 1).astype(F32)

    def moment_row(j, carry):
        g = jnp.broadcast_to(gs[pl.ds(j, 1), :], (16, WIDE))
        place = jnp.where(sub < 2, 1.0, jnp.where(sub < 4, (j - 8).astype(F32), cell_col))
        weight = jnp.where(sub < 6, g * place, 0.0)
        high = weight.astype(BF).astype(F32)
        weight = jnp.where((sub & 1) == 0, high, weight - high).astype(BF)
        weight = jnp.concatenate([weight, jnp.zeros((CH - 16, WIDE), BF)], axis=0)
        acc[...] += dot_nt(qb[j], weight)
        return carry

    lax.fori_loop(0, 24, moment_row, 0)
    sums = acc[...]

    def column_of(k):
        return jnp.broadcast_to(sums[:, k : k + 1], (tokens, CH))

    token = lax.broadcasted_iota(jnp.int32, (tokens, CH), 0)
    mass = column_of(0) + column_of(1)
    flow_row = (column_of(2) + column_of(3)) / mass - (token >> 6).astype(F32)
    own_col = (token & (COLS - 1)) + t * COLS
    flow_col = (column_of(4) + column_of(5)) / mass - own_col.astype(F32)

    left, right = placement(10, 1, 0), placement(10, 1, 1)
    for it in range(3):
        e = it + 1
        wait_halo(e)
        hp[it, :, 0:16] = dot(left, sx[e, 0].reshape(48, CH)).astype(BF).reshape(10, 16, CH)
        hp[it, :, 80:96] = dot(right, sx[e, 1].reshape(48, CH)).astype(BF).reshape(10, 16, CH)
        taps = jnp.concatenate([hp[it, 0:8], hp[it, 1:9], hp[it, 2:10]], axis=2)
        y = dot(taps.reshape(BAND * PADW, 3 * CH), wh[...])
        gate = roll0(y[:, : 2 * CH], 1) + y[:, 2 * CH : 4 * CH] + roll0(y[:, 4 * CH :], -1)
        gate = gate.reshape(BAND, PADW, 2 * CH)[:, 16:80].reshape(tokens, 2 * CH)

        def pushed(part):
            lanes = slice(part * CH, (part + 1) * CH)
            return (
                drive[:, lanes] + flow_row * mgate_w[0:1, lanes] + flow_col * mgate_w[1:2, lanes]
            )

        update = 0.5 * jnp.tanh(0.5 * (gate[:, :CH] + pushed(0))) + 0.5
        reset = 0.5 * jnp.tanh(0.5 * (gate[:, CH:] + pushed(1))) + 0.5
        hidden = hp[it, 1:9, 16:80].reshape(tokens, CH).astype(F32)
        candidate = jnp.tanh(dot((reset * hidden).astype(BF), cand_w[...]) + pushed(2))
        state = ((1.0 - update) * hidden + update * candidate).astype(BF)
        if it < 2:
            share(e + 1, state)
        step = dot(jnp.concatenate([state, state, state], axis=1), hw[...])
        flow_row = flow_row + step[:, :CH]
        flow_col = flow_col + step[:, CH:]
        if it == 2:
            hidden_out[...] = state.reshape(BAND, COLS, CH)

    lane = lax.broadcasted_iota(jnp.int32, (tokens, CH), 1)
    both = jnp.where(lane == 0, flow_row, flow_col)
    for q in range(4):
        turned = jnp.transpose(both[CH * q : CH * (q + 1)])
        for k in range(2):
            motion_out[k, 2 * q : 2 * q + 1, :] = turned[k : k + 1, 0:COLS]
            motion_out[k, 2 * q + 1 : 2 * q + 2, :] = turned[k : k + 1, COLS:CH]

    for w in range(2):
        for d in (0, 1, -1, 2, -2):
            if w == 0 and d == 0:
                continue

            @pl.when(row_ok(d))
            def _():
                raw_copy(w, d, t).wait_send()

        for chunk in range(3):
            fwd_copy(w, chunk, far if w else t).wait_send()
    for e in range(4):
        end_halo(e)
    for copy in col_copies:
        copy.wait_send()


def on_device(n_rows, *args):
    vmem = pl.BlockSpec(memory_space=pltpu.VMEM)
    smem = pl.BlockSpec(memory_space=pltpu.SMEM)
    tokens = BAND * COLS
    dma = pltpu.SemaphoreType.DMA
    return pl.pallas_call(
        functools.partial(kernel, n_rows),
        out_shape=(
            jax.ShapeDtypeStruct((2, BAND, COLS), F32),
            jax.ShapeDtypeStruct((BAND, COLS, CH), BF),
        ),
        in_specs=[vmem, smem] + [vmem] * 7,
        out_specs=(vmem, vmem),
        scratch_shapes=[
            pltpu.VMEM((4, 28, 32, CH), BF),
            pltpu.VMEM((28, WIDE, CH), BF),
            pltpu.VMEM((24, WIDE, CH), BF),
            pltpu.VMEM((24, tokens, WIDE), F32),
            pltpu.VMEM((24, tokens, WIDE), BF),
            pltpu.VMEM((12, PADW, CH), BF),
            pltpu.VMEM((12, PADW, CH), BF),
            pltpu.VMEM((3, 10, PADW, CH), BF),
            pltpu.VMEM((4, 2, 16, CH), BF),
            pltpu.VMEM((4, 2, 3, 16, CH), BF),
            pltpu.VMEM((2, 24, WIDE), F32),
            pltpu.VMEM((3, 2, 24, WIDE), F32),
            pltpu.VMEM((24, WIDE), F32),
            pltpu.VMEM((3, tokens, CH), F32),
            pltpu.VMEM((3, tokens, CH), F32),
            pltpu.VMEM((tokens, CH), BF),
            pltpu.VMEM((tokens, 3 * CH), F32),
            pltpu.VMEM((3 * CH, 3 * CH), BF),
            pltpu.VMEM((3 * CH, 6 * CH), BF),
            pltpu.VMEM((3 * CH, 2 * CH), BF),
            pltpu.VMEM((tokens, CH), F32),
            dma((2, 5)),
            dma((2, 5)),
            dma((2, 3)),
            dma((2, 3)),
            dma((4, 8)),
            dma((4, 8)),
            dma((3,)),
            dma((3,)),
        ],
        compiler_params=pltpu.CompilerParams(
            collective_id=0, has_side_effects=True, vmem_limit_bytes=52 * 1024 * 1024
        ),
    )(*args)


def solution(mesh):
    in_specs = (P("rows", "tgt", None), P("rows", None), P(), P(), P(), P(), P(), P(), P())
    out_specs = (P(None, "rows", "tgt"), P("rows", "tgt", None))
    return jax.shard_map(
        functools.partial(on_device, mesh.shape["rows"]),
        mesh=mesh,
        in_specs=in_specs,
        out_specs=out_specs,
        check_vma=False,
    )
```

time: 198 us -> 66.1 us (0.33)
  starting transfers between devices: 67.2 us -> 0 us
  Pallas kernels: 0 us -> 59.3 us
  matrix products: 41.2 us -> 0 us
  blocking collectives: 28.7 us -> 0 us
  waiting for transfers between devices: 27.9 us -> 0 us
  other arithmetic: 24.3 us -> 0 us
    ppermute x18 -> x0, starting transfers between devices: 67.2 us -> none  [the longest x8 30.5 us: extended(): after = lax.ppermute(initial, axis, down)]
    pallas_call x0 -> x1, Pallas kernels: none -> 59.3 us  [on_device(): pl.pallas_call(functools.partial(kernel, n_rows), out_shape=(jax.ShapeDty...]
    dot_general x51 -> x0, matrix products: 41.2 us -> none  [the longest x3 22.4 us: on_device(): moment = moment + jnp.dot(coupling, coords, precision=lax.Precision.HIGHEST)]
    ppermute x18 -> x0, waiting for transfers between devices: 27.9 us -> none  [the longest x8 14.7 us: extended(): before = lax.ppermute(last, axis, up)]
    reduce_sum x5 -> x0, other arithmetic: 13.3 us -> none  [the longest x1 6.95 us: on_device(): row_mass = jnp.sum(coupling, axis=1)]
    psum x1 -> x0, blocking collectives: 11.5 us -> none  [on_device(): sum_all = lax.psum(col_sum * jnp.exp(col_peak - top_all), 'tgt')]
    pmax x1 -> x0, blocking collectives: 10.9 us -> none  [on_device(): top_all = lax.pmax(col_peak, 'tgt')]
    all_gather x1 -> x0, blocking collectives: 6.39 us -> none  [on_device(): wide_band = lax.all_gather(target, 'tgt', axis=1, tiled=True)]
  transfers between devices with their start and end apart: 18 -> 0, of which waited for: 8 -> 0; matrix products, arithmetic and copies ran while one was open for 7% -> 0% of each run, Pallas kernels for 0% -> 0%
where the time goes in v1:
time: 66.1 us; the launch traced here: 65.9 us
  Pallas kernels  59.3 us (90%)
  local copies, waits for them, and re-layouts  5.9 us (9%)
  between operations  0.71 us (1%)
    pallas_call x1, Pallas kernels, on_device(): pl.pallas_call(functools.partial(kernel, n_rows), out_shape=(jax.ShapeDty...  59.3 us
    unnamed x19, local copies, waits for them, and re-layouts  5.9 us

profile of v1, /device:TPU:25, one launch (start us, length us, event | category | flops | bytes accessed | tf_op | source)
XLA Modules:
  0.0 65.9 jit_solution(10923095632339281362)
XLA Ops:
  0.6 0.0 copy-start.6
  0.6 0.0 copy-start.4
  0.7 0.0 copy-start.5
  0.7 0.0 copy-start.7
  0.7 0.8 %copy.11.mhead_w = f32[128,2]{1,0:T(8,128)S(1)} copy(f32[128,2]{0,1:T(2,128)} %param.17) | data formatting | bytes 2048 | tf_op args[8]
  1.5 0.0 copy-done.6
  1.5 0.0 copy-done.4
  1.5 0.0 copy-done.5
  1.5 0.0 copy-done.7
  1.5 0.0 copy-start
  1.5 1.1 %copy-done = bf16[9,128,256]{2,1,0:T(8,128)(2,1)S(1)} copy-done((bf16[9,128,256]{2,1,0:T(8,128)(2,1)S(1)}, bf16[9,128,256]{2,1,0:T(8,128)(2,1)}, u32[]{:S(2)}) %copy-start) | copy-done | bytes 589848
  2.6 0.0 copy-start.1
  2.6 1.0 %copy-done.1 = bf16[9,128,128]{2,1,0:T(8,128)(2,1)S(1)} copy-done((bf16[9,128,128]{2,1,0:T(8,128)(2,1)S(1)}, bf16[9,128,128]{2,1,0:T(8,128)(2,1)}, u32[]{:S(2)}) %copy-start.1) | copy-done | bytes 294936
  3.5 0.0 copy-start.2
  3.5 0.9 %copy-done.2 = bf16[8,64,128]{2,1,0:T(8,128)(2,1)S(1)} copy-done((bf16[8,64,128]{2,1,0:T(8,128)(2,1)S(1)}, bf16[8,64,128]{2,1,0:T(8,128)(2,1)}, u32[]{:S(2)}) %copy-start.2) | copy-done | bytes 131096
  4.4 0.0 copy-start.3
  4.5 0.9 %copy-done.3 = bf16[128,384]{1,0:T(8,128)(2,1)S(1)} copy-done((bf16[128,384]{1,0:T(8,128)(2,1)S(1)}, bf16[128,384]{1,0:T(8,128)(2,1)}, u32[]{:S(2)}) %copy-start.3) | copy-done | bytes 98328
  5.3 59.3 %shard_map.104 = (f32[2,8,64]{2,1,0:T(8,128)S(1)}, bf16[8,64,128]{2,1,0:T(8,128)(2,1)S(1)}) custom-call(bf16[8,64,128]{2,1,0:T(8,128)(2,1)S(1)} %copy-done.2, s32[1,3]{1,0:T(1,128)S(1)} %copy-done.7, bf16[64,128]{1,0:T(8,128)(2,1)S(1)} %copy-done.5, bf16[9,128,128]{2,1,0:T(8,128)(2,1)S(1)} %copy-done.1, bf16[128,384]{1,0:T(8,128)(2,1)S(1)} %copy-done.3, ...), custom_call_target="tpu_custom_call" | custom-call | tf_op jit(solution)/shard_map/pallas_call | solution.py:506
  64.6 0.6 copy.14
  65.2 0.7 copy.15
Async XLA Ops:
  0.6 0.9 %copy-start.6 = (f32[2,384]{1,0:T(2,128)S(1)}, f32[2,384]{1,0:T(2,128)}, u32[]{:S(2)}) copy-start(f32[2,384]{1,0:T(2,128)} %mgate_w.1) | copy-start | bytes 9220
  0.6 0.8 %copy-start.4 = (bf16[128,128]{1,0:T(8,128)(2,1)S(1)}, bf16[128,128]{1,0:T(8,128)(2,1)}, u32[]{:S(2)}) copy-start(bf16[128,128]{1,0:T(8,128)(2,1)} %cand_w.1) | copy-start | bytes 98308
  0.7 0.8 %copy-start.5 = (bf16[64,128]{1,0:T(8,128)(2,1)S(1)}, bf16[64,128]{1,0:T(8,128)(2,1)}, u32[]{:S(2)}) copy-start(bf16[64,128]{1,0:T(8,128)(2,1)} %patch_w.1) | copy-start | bytes 49156
  0.7 0.8 %copy-start.7 = (s32[1,3]{1,0:T(1,128)S(1)}, s32[1,3]{1,0:T(1,128)}, u32[]{:S(2)}) copy-start(s32[1,3]{1,0:T(1,128)} %window.1) | copy-start | bytes 40
  1.5 1.1 %copy-start = (bf16[9,128,256]{2,1,0:T(8,128)(2,1)S(1)}, bf16[9,128,256]{2,1,0:T(8,128)(2,1)}, u32[]{:S(2)}) copy-start(bf16[9,128,256]{2,1,0:T(8,128)(2,1)} %gate_w.1) | copy-start | bytes 1769476
  2.6 1.0 %copy-start.1 = (bf16[9,128,128]{2,1,0:T(8,128)(2,1)S(1)}, bf16[9,128,128]{2,1,0:T(8,128)(2,1)}, u32[]{:S(2)}) copy-start(bf16[9,128,128]{2,1,0:T(8,128)(2,1)} %dil_w.1) | copy-start | bytes 884740
  3.5 0.9 %copy-start.2 = (bf16[8,64,128]{2,1,0:T(8,128)(2,1)S(1)}, bf16[8,64,128]{2,1,0:T(8,128)(2,1)}, u32[]{:S(2)}) copy-start(bf16[8,64,128]{2,1,0:T(8,128)(2,1)} %frames.1) | copy-start | bytes 393220
  4.4 0.9 %copy-start.3 = (bf16[128,384]{1,0:T(8,128)(2,1)S(1)}, bf16[128,384]{1,0:T(8,128)(2,1)}, u32[]{:S(2)}) copy-start(bf16[128,384]{1,0:T(8,128)(2,1)} %ctx_w.1) | copy-start | bytes 294916

commit v2 on v1

v2 whole, which is shorter than its diff:
```python
import functools
import math

import jax
import jax.numpy as jnp
from jax import lax
from jax.experimental import pallas as pl
from jax.experimental.pallas import tpu as pltpu
from jax.sharding import PartitionSpec as P

BF = jnp.bfloat16
F32 = jnp.float32
LOG2E = 1.4426950408889634
BAND = 8
COLS = 64
WIDE = 256
CH = 128
PADW = 96
TOKENS = BAND * COLS
LIMIT = 63 * 1024 * 1024
CHUNK = 4 * WIDE


def roll0(x, shift):
    return pltpu.roll(x, shift % x.shape[0], axis=0)


def dot(a, b):
    return jnp.dot(a, b, preferred_element_type=F32)


def dot_nt(a, b):
    return lax.dot_general(a, b, (((1,), (1,)), ((), ())), preferred_element_type=F32)


def one_hot(rows, width, halo, side):
    token = lax.broadcasted_iota(jnp.int32, (rows * width, 48), 0)
    strip = lax.broadcasted_iota(jnp.int32, (rows * width, 48), 1)
    row, col = token // width, token % width
    base = 2 * (row + 8 - halo)
    if width == 16:
        hit = (col >= 14) & (strip == base + col - 14) if side == 0 else (col < 2) & (strip == base + col)
    else:
        hit = (col == 0) & (strip == base + 1) if side == 0 else (col == width - 1) & (strip == base)
    return jnp.where(hit, 1.0, 0.0).astype(BF)


def strip_pick():
    strip = lax.broadcasted_iota(jnp.int32, (32, TOKENS), 0)
    token = lax.broadcasted_iota(jnp.int32, (32, TOKENS), 1)
    row, col = (strip & 15) >> 1, strip & 1
    wanted = row * COLS + col + jnp.where(strip >= 16, COLS - 2, 0)
    return jnp.where(token == wanted, 1.0, 0.0).astype(BF)


def lanes_of(x, times):
    return jnp.concatenate([x] * times, axis=1)


def kernel(
    n_rows,
    frames_in,
    window,
    patch_in,
    dil_in,
    ctx_in,
    gate_in,
    cand_in,
    mgate_in,
    mhead_in,
    motion_out,
    hidden_out,
    frames,
    patch_w,
    dil_w,
    ctx_w,
    gate_w,
    cand_w,
    mgate_w,
    mhead_w,
    pk,
    raw,
    e1,
    f1,
    sb,
    qb,
    rp,
    e0,
    hp,
    sbuf,
    sx,
    st,
    sr,
    cmax,
    rowmax,
    rowsum,
    pot,
    f0,
    drive,
    gpre,
    flow,
    wc,
    hw,
    acc,
    in_sem,
    raw_send,
    raw_recv,
    feat_send,
    feat_recv,
    halo_send,
    halo_recv,
    col_send,
    col_recv,
):
    r = lax.axis_index("rows")
    t = lax.axis_index("tgt")
    core = t % 2
    sib = t + 1 - 2 * core
    far = (t + 2) % 4
    far_sib = 3 - t
    away = 2 * core - 1

    loads = {}
    for k, (src, dst) in enumerate(
        (
            (frames_in, frames),
            (patch_in, patch_w),
            (dil_in, dil_w),
            (ctx_in, ctx_w),
            (gate_in, gate_w),
            (cand_in, cand_w),
            (mgate_in, mgate_w),
            (mhead_in, mhead_w),
        )
    ):
        loads[k] = pltpu.make_async_copy(src, dst, in_sem.at[k])
        loads[k].start()

    def row_ok(d):
        return (r + d >= 0) & (r + d < n_rows)

    def col_ok(d):
        return (t + d >= 0) & (t + d < 4)

    def remote(src, dst, send, recv, rr, tt):
        return pltpu.make_async_remote_copy(
            src_ref=src,
            dst_ref=dst,
            send_sem=send,
            recv_sem=recv,
            device_id=(rr, tt),
            device_id_type=pl.DeviceIdType.MESH,
        )

    barrier = pltpu.get_barrier_semaphore()
    count = 3

    def greet(rr, tt):
        pl.semaphore_signal(
            barrier, inc=1, device_id=(rr, tt), device_id_type=pl.DeviceIdType.MESH
        )

    for d in (1, -1):

        @pl.when(row_ok(d))
        def _():
            for tt in range(4):
                greet(r + d, tt)

        count = count + 4 * row_ok(d).astype(jnp.int32)

    @pl.when(row_ok(2 * away))
    def _():
        for tt in range(4):
            greet(r + 2 * away, tt)

    for d in (2, -2):
        count = count + 2 * row_ok(d).astype(jnp.int32)
    for tt in (far, sib, far_sib):
        greet(r, tt)

    def zero(ref):
        ref[...] = jnp.zeros(ref.shape, ref.dtype)

    near_row, next_row, own_row = 2 + 4 * core, 14 * core, 10 * (1 - core)
    for d, first, n in ((away, near_row, 8), (2 * away, next_row, 2)):

        @pl.when(jnp.logical_not(row_ok(d)))
        def _():
            for b in range(4):
                zero(raw.at[b, pl.ds(first, n)])

    for d, rp_lo, rp_hi, hp_row, slot in ((-1, 0, 2, 0, 0), (1, 10, 12, 9, 2)):

        @pl.when(jnp.logical_not(row_ok(d)))
        def _():
            rp[rp_lo:rp_hi, 16:80] = jnp.zeros((2, COLS, CH), BF)
            for e in range(3):
                hp[e, hp_row] = jnp.zeros((COLS, CH), BF)
            for e in range(4):
                for side in range(2):
                    zero(sx.at[e, side, slot])

    for d, side in ((-1, 0), (1, 1)):

        @pl.when(jnp.logical_not(col_ok(d)))
        def _():
            for e in range(4):
                for slot in range(3):
                    zero(sx.at[e, side, slot])

    loads[0].wait()
    whole = frames[...].astype(F32)
    half0 = whole[:, 0:32].reshape(BAND * 32, CH)
    half1 = whole[:, 32:64].reshape(BAND * 32, CH)
    lane = lax.broadcasted_iota(jnp.int32, (BAND * 32, CH), 1)
    packed = jnp.where(lane < 64, pltpu.roll(half0, 64, axis=1), half1)
    pk[...] = packed.astype(BF).reshape(BAND, 32, CH)
    raw[t, pl.ds(own_row, 6)] = pk[pl.ds(2 * core, 6)]
    pick = strip_pick()
    sbuf[0] = dot(pick, frames[...].reshape(TOKENS, CH)).astype(BF).reshape(2, 16, CH)

    pl.semaphore_wait(barrier, count)

    def raw_copy(src, dst, k, kind, rr, tt):
        return remote(src, dst, raw_send.at[k], raw_recv.at[t, kind], rr, tt)

    raw_sends = []
    k = 0
    for peer, c in ((far, core), (far_sib, 1 - core), (sib, 1 - core)):
        src, dst = pk.at[pl.ds(2 * c, 6)], raw.at[t, pl.ds(10 * (1 - c), 6)]
        raw_sends.append((None, raw_copy(src, dst, k, 0, r, peer)))
        k += 1
    for peer in (0, 2):
        raw_sends.append((1, raw_copy(pk, raw.at[t, 2:10], k, 1, r + 1, peer)))
        raw_sends.append((-1, raw_copy(pk, raw.at[t, 6:14], k + 1, 1, r - 1, peer + 1)))
        k += 2
    for peer in (0, 2):
        raw_sends.append((2, raw_copy(pk.at[6:8], raw.at[t, 0:2], k, 2, r + 2, peer)))
        raw_sends.append((-2, raw_copy(pk.at[0:2], raw.at[t, 14:16], k + 1, 2, r - 2, peer + 1)))
        k += 2

    def when_row(d, act):
        if d is None:
            act()
        else:
            pl.when(row_ok(d))(act)

    for d, copy in raw_sends:
        when_row(d, copy.start)

    def wait_raw(b):
        @pl.when(b != t)
        def _():
            ref = raw.at[b, pl.ds(own_row, 6)]
            remote(ref, ref, raw_send.at[0], raw_recv.at[b, 0], r, sib).wait_recv()

        @pl.when(row_ok(away))
        def _():
            ref = raw.at[b, pl.ds(near_row, 8)]
            remote(ref, ref, raw_send.at[0], raw_recv.at[b, 1], r, sib).wait_recv()

        @pl.when(row_ok(2 * away))
        def _():
            ref = raw.at[b, pl.ds(next_row, 2)]
            remote(ref, ref, raw_send.at[0], raw_recv.at[b, 2], r, sib).wait_recv()

    def halo_copies(e):
        copies = []
        for d in (1, -1):
            if e == 0:
                src = frames.at[6:8] if d == 1 else frames.at[0:2]
                dst = rp.at[0:2, 16:80] if d == 1 else rp.at[10:12, 16:80]
            else:
                src = hp.at[e - 1, 8] if d == 1 else hp.at[e - 1, 1]
                dst = hp.at[e - 1, 0] if d == 1 else hp.at[e - 1, 9]
            copies.append((d, 0, src, dst))
        for dt in (-1, 1):
            own = 0 if dt == -1 else 1
            for d in (1, -1, 0):
                copies.append((d, dt, sbuf.at[e, own], sx.at[e, 1 - own, 1 - d]))
        return [
            (d, dt, remote(src, dst, halo_send.at[e, k], halo_recv.at[e, k], r + d, t + dt))
            for k, (d, dt, src, dst) in enumerate(copies)
        ]

    def start_halo(e):
        for d, dt, copy in halo_copies(e):
            pl.when(row_ok(d) & col_ok(dt))(copy.start)

    def wait_halo(e):
        for d, dt, copy in halo_copies(e):
            pl.when(row_ok(-d) & col_ok(-dt))(copy.wait_recv)

    def end_halo(e):
        for d, dt, copy in halo_copies(e):
            pl.when(row_ok(d) & col_ok(dt))(copy.wait_send)

    start_halo(0)

    for k in range(1, 8):
        loads[k].wait()
    for a in range(3):
        for b in range(3):
            wc[a * CH : (a + 1) * CH, b * CH : (b + 1) * CH] = dil_w[3 * a + b]
    for k in range(2):
        column = jnp.transpose(jnp.broadcast_to(mhead_w[k : k + 1, :], (CH, CH)))
        for part in range(3):
            rounded = column.astype(BF)
            hw[part * CH : (part + 1) * CH, k * CH : (k + 1) * CH] = rounded
            column = column - rounded.astype(F32)
    embed_one = jnp.concatenate([patch_w[...], jnp.zeros((64, CH), BF)], axis=0)
    embed_two = jnp.concatenate(
        [embed_one, jnp.concatenate([jnp.zeros((64, CH), BF), patch_w[...]], axis=0)], axis=1
    )
    rp[2:10, 16:80] = frames[...]

    place0, place1 = one_hot(12, 16, 2, 0), one_hot(12, 16, 2, 1)
    wait_halo(0)
    rp[:, 0:16] = dot(place0, sx[0, 0].reshape(48, CH)).astype(BF).reshape(12, 16, CH)
    rp[:, 80:96] = dot(place1, sx[0, 1].reshape(48, CH)).astype(BF).reshape(12, 16, CH)
    e0[...] = dot(rp[...].reshape(12 * PADW, CH), embed_one).astype(BF).reshape(12, PADW, CH)
    flat = e0[...].reshape(12 * PADW, CH).astype(F32)
    middle = e0[:, 16:80]

    def moved(shift):
        return roll0(flat, shift).reshape(12, PADW, CH)[:, 16:80].astype(BF)

    shifted = (moved(2), middle, moved(-2))
    taps = [shifted[b][2 * a : 2 * a + 8].reshape(TOKENS, CH) for a in range(3) for b in range(3)]
    conv = dot(jnp.concatenate(taps, axis=1), dil_w[...].reshape(9 * CH, CH))
    own = middle[2:10].reshape(TOKENS, CH).astype(F32)
    features = (own + jnp.maximum(conv, 0.0)).astype(BF)
    f0[...] = features
    drive[...] = dot(features, ctx_w[...])

    def share(e, state):
        hp[e - 1, 1:9] = state.reshape(BAND, COLS, CH)
        sbuf[e] = dot(pick, state).astype(BF).reshape(2, 16, CH)
        start_halo(e)

    share(1, jnp.tanh(features.astype(F32)).astype(BF))

    for b in range(4):
        wait_raw(b)
        pair = dot(raw[b].reshape(16 * 32, CH), embed_two).astype(BF)
        e1[:, b * COLS : b * COLS + 32] = pair[:, :CH].reshape(16, 32, CH)
        e1[:, b * COLS + 32 : b * COLS + 64] = pair[:, CH:].reshape(16, 32, CH)

    column = lax.broadcasted_iota(jnp.int32, (CHUNK, CH), 0) & (WIDE - 1)
    feat_copies = [
        remote(f1.at[3 * core + i], f1.at[3 * core + i], feat_send.at[i], feat_recv.at[i], r, sib)
        for i in range(3)
    ]
    for i in range(3):
        rows = [e1[4 * i + 2 * a : 4 * i + 2 * a + 4] for a in range(3)]
        y = dot(jnp.concatenate(rows, axis=2).reshape(CHUNK, 3 * CH), wc[...])
        before = jnp.where(column < 2, 0.0, roll0(y[:, :CH], 2))
        after = jnp.where(column >= WIDE - 2, 0.0, roll0(y[:, 2 * CH :], -2))
        conv = before + y[:, CH : 2 * CH] + after
        own = rows[1].reshape(CHUNK, CH).astype(F32)
        f1[3 * core + i] = (own + jnp.maximum(conv, 0.0)).astype(BF)
        feat_copies[i].start()

    scale = LOG2E / math.sqrt(CH)
    rowmax[...] = jnp.full(rowmax.shape, -jnp.inf, F32)
    rowsum[...] = jnp.zeros(rowsum.shape, F32)

    def score_chunk(c):
        peak = rowmax[c // 2]
        for n in range(4):
            s = dot_nt(f0[...], f1[c, n * WIDE : (n + 1) * WIDE]) * scale
            sb[c, :, n * WIDE : (n + 1) * WIDE] = s
            peak = jnp.maximum(peak, jnp.maximum(s[:, :CH], s[:, CH:]))
        rowmax[c // 2] = peak

    def own_scores(i, carry):
        score_chunk(3 * core + i)
        return carry

    lax.fori_loop(0, 3, own_scores, 0)
    for i in range(3):
        c = 3 * (1 - core) + i
        remote(f1.at[c], f1.at[c], feat_send.at[i], feat_recv.at[i], r, sib).wait_recv()

    def other_scores(i, carry):
        score_chunk(3 * (1 - core) + i)
        return carry

    lax.fori_loop(0, 3, other_scores, 0)

    allowed = []
    for o in range(3):
        ok = (window[0, o] == 1) & row_ok(o - 1)
        allowed.append(ok.astype(jnp.int32))

    def picked(o, x, other):
        return jnp.where(jnp.full(x.shape, allowed[o]) == 1, x, other)

    top = None
    for o in range(3):
        peak = jnp.broadcast_to(jnp.max(rowmax[o], axis=1, keepdims=True), (TOKENS, CH))
        peak = picked(o, peak, -jnp.inf)
        top = peak if top is None else jnp.maximum(top, peak)
    pot[0] = top

    rb = 32

    def eighths(x):
        return x.reshape(rb // 8, 8, CHUNK)

    def mass_chunk(c, carry):
        def block(k, col):
            i = pl.multiple_of(k * rb, rb)
            x = sb[c, pl.ds(i, rb), :] - lanes_of(pot[0, pl.ds(i, rb), :], 8)
            p = jnp.exp2(x)
            parts = [p[:, n * CH : (n + 1) * CH] for n in range(8)]
            while len(parts) > 1:
                parts = [a + b for a, b in zip(parts[::2], parts[1::2])]
            rowsum[c // 2, pl.ds(i, rb), :] += parts[0]
            return jnp.maximum(col, jnp.max(eighths(x), axis=0))

        col = lax.fori_loop(0, TOKENS // rb, block, jnp.full((8, CHUNK), -jnp.inf, F32), unroll=2)
        cmax[c] = jnp.broadcast_to(jnp.max(col, axis=0, keepdims=True), (8, CHUNK))
        return carry

    lax.fori_loop(0, 6, mass_chunk, 0)
    total = None
    for o in range(3):
        part = picked(o, rowsum[o], 0.0)
        total = part if total is None else total + part
    total = jnp.broadcast_to(jnp.sum(total, axis=1, keepdims=True), (TOKENS, CH))
    pot[1] = pot[0] + jnp.log(total) * LOG2E

    def col_chunk(c):
        def block(k, col):
            i = pl.multiple_of(k * rb, rb)
            x = sb[c, pl.ds(i, rb), :] - lanes_of(pot[1, pl.ds(i, rb), :], 8)
            q = jnp.exp2(x - cmax[c, 0:1, :])
            qb[c, pl.ds(i, rb), :] = q.astype(BF)
            return col + jnp.sum(eighths(q), axis=0)

        col = lax.fori_loop(0, TOKENS // rb, block, jnp.zeros((8, CHUNK), F32), unroll=2)
        st[c, 0:1] = cmax[c, 0:1]
        st[c, 1:2] = jnp.sum(col, axis=0, keepdims=True)

    peers = (sib, far, far_sib)

    def col_copy(k, c):
        return remote(st.at[c], sr.at[k, c], col_send.at[k, c], col_recv.at[k, c], r, peers[k])

    def col_step(c, carry):
        col_chunk(c)
        for k in (1, 2, 0):
            col_copy(k, c).start()
        return carry

    lax.fori_loop(0, 6, col_step, 0)

    left, right = one_hot(10, COLS, 1, 0), one_hot(10, COLS, 1, 1)
    edge = lax.broadcasted_iota(jnp.int32, (10 * COLS, CH), 0) & (COLS - 1)

    def gate_conv(e):
        wait_halo(e)
        state = hp[e - 1].reshape(10 * COLS, CH)
        wide = state.astype(F32)
        before = jnp.where(edge == 0, dot(left, sx[e, 0].reshape(48, CH)), roll0(wide, 1))
        after = jnp.where(edge == COLS - 1, dot(right, sx[e, 1].reshape(48, CH)), roll0(wide, -1))
        shifted = (before.astype(BF), state, after.astype(BF))
        taps = [shifted[b][a * COLS : a * COLS + TOKENS] for a in range(3) for b in range(3)]
        conv = dot(jnp.concatenate(taps, axis=1), gate_w[...].reshape(9 * CH, 2 * CH))
        gpre[...] = conv + drive[:, : 2 * CH]

    gate_conv(1)

    sub = lax.broadcasted_iota(jnp.int32, (16, CHUNK), 0)
    cell = lax.broadcasted_iota(jnp.int32, (16, CHUNK), 1)
    cell_row = (cell >> 8).astype(F32)
    cell_col = (cell & (WIDE - 1)).astype(F32)
    acc[...] = jnp.zeros(acc.shape, F32)

    def moment_chunk(c, carry):
        for k in range(3):
            col_copy(k, c).wait_recv()
        peak = jnp.maximum(
            jnp.maximum(st[c, 0:1], sr[0, c, 0:1]), jnp.maximum(sr[1, c, 0:1], sr[2, c, 0:1])
        )
        mine = jnp.exp2(st[c, 0:1] - peak)
        total = st[c, 1:2] * mine
        for k in range(3):
            total = total + sr[k, c, 1:2] * jnp.exp2(sr[k, c, 0:1] - peak)
        factor = mine / total
        open_band = jnp.where(
            c < 2, allowed[0], jnp.where(c < 4, allowed[1], allowed[2])
        )
        factor = jnp.where(jnp.full((1, CHUNK), open_band) == 1, factor, 0.0)
        g = jnp.broadcast_to(factor, (16, CHUNK))
        place = jnp.where(sub < 2, 1.0, jnp.where(sub < 4, cell_row + (4 * c - 8).astype(F32), cell_col))
        weight = jnp.where(sub < 6, g * place, 0.0)
        high = weight.astype(BF).astype(F32)
        weight = jnp.where((sub & 1) == 0, high, weight - high).astype(BF)
        weight = jnp.concatenate([weight, jnp.zeros((CH - 16, CHUNK), BF)], axis=0)
        acc[...] += dot_nt(qb[c], weight)
        return carry

    lax.fori_loop(0, 6, moment_chunk, 0)
    sums = acc[...]

    def column_of(k):
        return jnp.broadcast_to(sums[:, k : k + 1], (TOKENS, CH))

    token = lax.broadcasted_iota(jnp.int32, (TOKENS, CH), 0)
    mass = column_of(0) + column_of(1)
    flow[0] = (column_of(2) + column_of(3)) / mass - (token >> 6).astype(F32)
    own_col = (token & (COLS - 1)) + t * COLS
    flow[1] = (column_of(4) + column_of(5)) / mass - own_col.astype(F32)

    for it in range(3):
        if it > 0:
            gate_conv(it + 1)
        part = 128
        states = []
        for q in range(TOKENS // part):
            at = slice(q * part, (q + 1) * part)
            flow_row, flow_col = flow[0, at], flow[1, at]

            def pushed(n):
                lanes = slice(n * CH, (n + 1) * CH)
                return flow_row * mgate_w[0:1, lanes] + flow_col * mgate_w[1:2, lanes]

            update = 0.5 * jnp.tanh(0.5 * (gpre[at, :CH] + pushed(0))) + 0.5
            reset = 0.5 * jnp.tanh(0.5 * (gpre[at, CH:] + pushed(1))) + 0.5
            hidden = hp[it, 1 + 2 * q : 3 + 2 * q].reshape(part, CH).astype(F32)
            candidate = dot((reset * hidden).astype(BF), cand_w[...])
            candidate = jnp.tanh(candidate + drive[at, 2 * CH :] + pushed(2))
            states.append(((1.0 - update) * hidden + update * candidate).astype(BF))
        state = jnp.concatenate(states, axis=0)
        if it < 2:
            share(it + 2, state)
        else:
            hidden_out[...] = state.reshape(BAND, COLS, CH)
        step = dot(jnp.concatenate([state, state, state], axis=1), hw[...])
        flow[0] += step[:, :CH]
        flow[1] += step[:, CH:]

    lane = lax.broadcasted_iota(jnp.int32, (TOKENS, CH), 1)
    both = jnp.where(lane == 0, flow[0], flow[1])
    for q in range(4):
        turned = jnp.transpose(both[CH * q : CH * (q + 1)])
        for k in range(2):
            motion_out[k, 2 * q : 2 * q + 1, :] = turned[k : k + 1, 0:COLS]
            motion_out[k, 2 * q + 1 : 2 * q + 2, :] = turned[k : k + 1, COLS:CH]

    for d, copy in raw_sends:
        when_row(d, copy.wait_send)
    for copy in feat_copies:
        copy.wait_send()
    for e in range(4):
        end_halo(e)

    def end_col(c, carry):
        for k in range(3):
            col_copy(k, c).wait_send()
        return carry

    lax.fori_loop(0, 6, end_col, 0)


def on_device(n_rows, *args):
    vmem = pl.BlockSpec(memory_space=pltpu.VMEM)
    smem = pl.BlockSpec(memory_space=pltpu.SMEM)
    hbm = pl.BlockSpec(memory_space=pl.ANY)
    dma = pltpu.SemaphoreType.DMA
    args = (*args[:8], args[8].T)
    inputs = [x for k, x in enumerate(args) if k != 1]
    return pl.pallas_call(
        functools.partial(kernel, n_rows),
        out_shape=(
            jax.ShapeDtypeStruct((2, BAND, COLS), F32),
            jax.ShapeDtypeStruct((BAND, COLS, CH), BF),
        ),
        in_specs=[hbm, smem] + [hbm] * 7,
        out_specs=(vmem, vmem),
        scratch_shapes=[pltpu.VMEM(x.shape, x.dtype) for x in inputs]
        + [
            pltpu.VMEM((BAND, 32, CH), BF),
            pltpu.VMEM((4, 16, 32, CH), BF),
            pltpu.VMEM((16, WIDE, CH), BF),
            pltpu.VMEM((6, CHUNK, CH), BF),
            pltpu.VMEM((6, TOKENS, CHUNK), F32),
            pltpu.VMEM((6, TOKENS, CHUNK), BF),
            pltpu.VMEM((12, PADW, CH), BF),
            pltpu.VMEM((12, PADW, CH), BF),
            pltpu.VMEM((3, 10, COLS, CH), BF),
            pltpu.VMEM((4, 2, 16, CH), BF),
            pltpu.VMEM((4, 2, 3, 16, CH), BF),
            pltpu.VMEM((6, 2, CHUNK), F32),
            pltpu.VMEM((3, 6, 2, CHUNK), F32),
            pltpu.VMEM((6, 8, CHUNK), F32),
            pltpu.VMEM((3, TOKENS, CH), F32),
            pltpu.VMEM((3, TOKENS, CH), F32),
            pltpu.VMEM((2, TOKENS, CH), F32),
            pltpu.VMEM((TOKENS, CH), BF),
            pltpu.VMEM((TOKENS, 3 * CH), F32),
            pltpu.VMEM((TOKENS, 2 * CH), F32),
            pltpu.VMEM((2, TOKENS, CH), F32),
            pltpu.VMEM((3 * CH, 3 * CH), BF),
            pltpu.VMEM((3 * CH, 2 * CH), BF),
            pltpu.VMEM((TOKENS, CH), F32),
            dma((8,)),
            dma((11,)),
            dma((4, 3)),
            dma((3,)),
            dma((3,)),
            dma((4, 8)),
            dma((4, 8)),
            dma((3, 6)),
            dma((3, 6)),
        ],
        compiler_params=pltpu.CompilerParams(
            collective_id=0, has_side_effects=True, vmem_limit_bytes=LIMIT
        ),
    )(*args)


def solution(mesh):
    in_specs = (P("rows", "tgt", None), P("rows", None), P(), P(), P(), P(), P(), P(), P())
    out_specs = (P(None, "rows", "tgt"), P("rows", "tgt", None))
    return jax.shard_map(
        functools.partial(on_device, mesh.shape["rows"]),
        mesh=mesh,
        in_specs=in_specs,
        out_specs=out_specs,
        check_vma=False,
    )
```

time: 66.1 us -> 52.2 us (0.79)
  Pallas kernels: 59.3 us -> 48.5 us
  local copies, waits for them, and re-layouts: 5.9 us -> 2.86 us
    pallas_call x1, Pallas kernels: 59.3 us -> 48.5 us  [on_device(): pl.pallas_call(functools.partial(kernel, n_rows), out_shape=(jax.ShapeDty...]
    unnamed x19 -> x2, local copies, waits for them, and re-layouts: 5.9 us -> 2.86 us
where the time goes in v2:
time: 52.2 us; the launch traced here: 52 us
  Pallas kernels  48.5 us (93%)
  local copies, waits for them, and re-layouts  2.86 us (5%)
  between operations  0.64 us (1%)
    pallas_call x1, Pallas kernels, on_device(): pl.pallas_call(functools.partial(kernel, n_rows), out_shape=(jax.ShapeDty...  48.5 us
    unnamed x2, local copies, waits for them, and re-layouts  2.86 us

profile of v2, /device:TPU:25, one launch (start us, length us, event | category | flops | bytes accessed | tf_op | source)
XLA Modules:
  0.0 52.0 jit_solution(10139273709047132781)
XLA Ops:
  0.6 48.5 %shard_map.104 = (f32[2,8,64]{2,1,0:T(8,128)}, bf16[8,64,128]{2,1,0:T(8,128)(2,1)}) custom-call(bf16[8,64,128]{2,1,0:T(8,128)(2,1)} %frames_in.1, s32[1,3]{1,0:T(1,128)} %window.1, bf16[64,128]{1,0:T(8,128)(2,1)} %patch_in.1, bf16[9,128,128]{2,1,0:T(8,128)(2,1)} %dil_in.1, bf16[128,384]{1,0:T(8,128)(2,1)} %ctx_in.1, bf16[9,128,256]{2,1,0:T(8,128)(2,1)} %gate_in.1, ...), custom_call_target="tpu_custom_call" | custom-call | tf_op jit(solution)/shard_map/pallas_call | solution.py:576
  49.2 1.3 %copy.13 = f32[2,8,64]{2,1,0:T(8,128)} copy(f32[2,8,64]{2,1,0:T(8,128)} %get-tuple-element.4) | data formatting | bytes 8192
  50.5 1.6 %copy.14 = bf16[8,64,128]{2,1,0:T(8,128)(2,1)} copy(bf16[8,64,128]{2,1,0:T(8,128)(2,1)} %get-tuple-element.5) | data formatting | bytes 262144

commit v3 on v2

--- a/solution.py
+++ b/solution.py
@@ -33,15 +33,15 @@
     return lax.dot_general(a, b, (((1,), (1,)), ((), ())), preferred_element_type=F32)
 
 
-def one_hot(rows, width, halo, side):
-    token = lax.broadcasted_iota(jnp.int32, (rows * width, 48), 0)
-    strip = lax.broadcasted_iota(jnp.int32, (rows * width, 48), 1)
-    row, col = token // width, token % width
+def one_hot(rows, halo, side):
+    token = lax.broadcasted_iota(jnp.int32, (rows * 16, 48), 0)
+    strip = lax.broadcasted_iota(jnp.int32, (rows * 16, 48), 1)
+    row, col = token >> 4, token & 15
     base = 2 * (row + 8 - halo)
-    if width == 16:
-        hit = (col >= 14) & (strip == base + col - 14) if side == 0 else (col < 2) & (strip == base + col)
+    if side == 0:
+        hit = (col >= 14) & (strip == base + col - 14)
     else:
-        hit = (col == 0) & (strip == base + 1) if side == 0 else (col == width - 1) & (strip == base)
+        hit = (col < 2) & (strip == base + col)
     return jnp.where(hit, 1.0, 0.0).astype(BF)
 
 
@@ -51,6 +51,13 @@
     row, col = (strip & 15) >> 1, strip & 1
     wanted = row * COLS + col + jnp.where(strip >= 16, COLS - 2, 0)
     return jnp.where(token == wanted, 1.0, 0.0).astype(BF)
+
+
+def side_pick(side):
+    row = lax.broadcasted_iota(jnp.int32, (48, 48), 0)
+    strip = lax.broadcasted_iota(jnp.int32, (48, 48), 1)
+    wanted = 2 * ((row & 7) + (row >> 4) + 7) + 1 - side
+    return jnp.where((strip == wanted) & ((row & 15) < 8), 1.0, 0.0).astype(BF)
 
 
 def lanes_of(x, times):
@@ -246,9 +253,6 @@
         else:
             pl.when(row_ok(d))(act)
 
-    for d, copy in raw_sends:
-        when_row(d, copy.start)
-
     def wait_raw(b):
         @pl.when(b != t)
         def _():
@@ -297,25 +301,21 @@
             pl.when(row_ok(d) & col_ok(dt))(copy.wait_send)
 
     start_halo(0)
+    for d, copy in raw_sends:
+        when_row(d, copy.start)
 
     for k in range(1, 8):
         loads[k].wait()
     for a in range(3):
         for b in range(3):
             wc[a * CH : (a + 1) * CH, b * CH : (b + 1) * CH] = dil_w[3 * a + b]
-    for k in range(2):
-        column = jnp.transpose(jnp.broadcast_to(mhead_w[k : k + 1, :], (CH, CH)))
-        for part in range(3):
-            rounded = column.astype(BF)
-            hw[part * CH : (part + 1) * CH, k * CH : (k + 1) * CH] = rounded
-            column = column - rounded.astype(F32)
     embed_one = jnp.concatenate([patch_w[...], jnp.zeros((64, CH), BF)], axis=0)
     embed_two = jnp.concatenate(
         [embed_one, jnp.concatenate([jnp.zeros((64, CH), BF), patch_w[...]], axis=0)], axis=1
     )
     rp[2:10, 16:80] = frames[...]
-
-    place0, place1 = one_hot(12, 16, 2, 0), one_hot(12, 16, 2, 1)
+    place0, place1 = one_hot(12, 2, 0), one_hot(12, 2, 1)
+
     wait_halo(0)
     rp[:, 0:16] = dot(place0, sx[0, 0].reshape(48, CH)).astype(BF).reshape(12, 16, CH)
     rp[:, 80:96] = dot(place1, sx[0, 1].reshape(48, CH)).astype(BF).reshape(12, 16, CH)
@@ -340,6 +340,13 @@
         start_halo(e)
 
     share(1, jnp.tanh(features.astype(F32)).astype(BF))
+
+    for k in range(2):
+        column = jnp.transpose(jnp.broadcast_to(mhead_w[k : k + 1, :], (CH, CH)))
+        for part in range(3):
+            rounded = column.astype(BF)
+            hw[part * CH : (part + 1) * CH, k * CH : (k + 1) * CH] = rounded
+            column = column - rounded.astype(F32)
 
     for b in range(4):
         wait_raw(b)
@@ -420,7 +427,7 @@
             rowsum[c // 2, pl.ds(i, rb), :] += parts[0]
             return jnp.maximum(col, jnp.max(eighths(x), axis=0))
 
-        col = lax.fori_loop(0, TOKENS // rb, block, jnp.full((8, CHUNK), -jnp.inf, F32), unroll=2)
+        col = lax.fori_loop(0, TOKENS // rb, block, jnp.full((8, CHUNK), -jnp.inf, F32), unroll=4)
         cmax[c] = jnp.broadcast_to(jnp.max(col, axis=0, keepdims=True), (8, CHUNK))
         return carry
 
@@ -440,7 +447,7 @@
             qb[c, pl.ds(i, rb), :] = q.astype(BF)
             return col + jnp.sum(eighths(q), axis=0)
 
-        col = lax.fori_loop(0, TOKENS // rb, block, jnp.zeros((8, CHUNK), F32), unroll=2)
+        col = lax.fori_loop(0, TOKENS // rb, block, jnp.zeros((8, CHUNK), F32), unroll=4)
         st[c, 0:1] = cmax[c, 0:1]
         st[c, 1:2] = jnp.sum(col, axis=0, keepdims=True)
 
@@ -457,21 +464,46 @@
 
     lax.fori_loop(0, 6, col_step, 0)
 
-    left, right = one_hot(10, COLS, 1, 0), one_hot(10, COLS, 1, 1)
-    edge = lax.broadcasted_iota(jnp.int32, (10 * COLS, CH), 0) & (COLS - 1)
-
-    def gate_conv(e):
-        wait_halo(e)
-        state = hp[e - 1].reshape(10 * COLS, CH)
-        wide = state.astype(F32)
-        before = jnp.where(edge == 0, dot(left, sx[e, 0].reshape(48, CH)), roll0(wide, 1))
-        after = jnp.where(edge == COLS - 1, dot(right, sx[e, 1].reshape(48, CH)), roll0(wide, -1))
-        shifted = (before.astype(BF), state, after.astype(BF))
-        taps = [shifted[b][a * COLS : a * COLS + TOKENS] for a in range(3) for b in range(3)]
+    edge = lax.broadcasted_iota(jnp.int32, (TOKENS, CH), 0) & (COLS - 1)
+    picks = (side_pick(0), side_pick(1))
+    border = jnp.zeros((COLS, CH), BF)
+
+    def beside(x, n):
+        wide, at = x.astype(F32), edge[:n]
+        before = jnp.where(at == 0, 0.0, roll0(wide, 1)).astype(BF)
+        after = jnp.where(at == COLS - 1, 0.0, roll0(wide, -1)).astype(BF)
+        return before, x, after
+
+    def own_gates(state):
+        taps = []
+        shifted = beside(state, TOKENS)
+        for a in range(3):
+            for x in shifted:
+                if a == 0:
+                    x = jnp.concatenate([border, x[: TOKENS - COLS]], axis=0)
+                elif a == 2:
+                    x = jnp.concatenate([x[COLS:], border], axis=0)
+                taps.append(x)
         conv = dot(jnp.concatenate(taps, axis=1), gate_w[...].reshape(9 * CH, 2 * CH))
         gpre[...] = conv + drive[:, : 2 * CH]
 
-    gate_conv(1)
+    def edge_gates(e):
+        wait_halo(e)
+        for a, row, at in ((0, 0, 0), (2, 9, TOKENS - COLS)):
+            x = jnp.concatenate(beside(hp[e - 1, row], COLS), axis=1)
+            w = gate_w[3 * a : 3 * a + 3].reshape(3 * CH, 2 * CH)
+            gpre[at : at + COLS] += dot(x, w)
+        for side, b, at in ((0, 0, 0), (1, 2, COLS - 1)):
+            x = dot(picks[side], sx[e, side].reshape(48, CH)).astype(BF)
+            x = jnp.concatenate([x[0:8], x[16:24], x[32:40]], axis=1)
+            w = jnp.concatenate([gate_w[b], gate_w[3 + b], gate_w[6 + b]], axis=0)
+            extra = dot(x, w)
+            for y in range(BAND):
+                i = y * COLS + at
+                gpre[i : i + 1] += extra[y : y + 1]
+
+    own_gates(hp[0, 1:9].reshape(TOKENS, CH))
+    edge_gates(1)
 
     sub = lax.broadcasted_iota(jnp.int32, (16, CHUNK), 0)
     cell = lax.broadcasted_iota(jnp.int32, (16, CHUNK), 1)
@@ -517,7 +549,7 @@
 
     for it in range(3):
         if it > 0:
-            gate_conv(it + 1)
+            edge_gates(it + 1)
         part = 128
         states = []
         for q in range(TOKENS // part):
@@ -542,6 +574,8 @@
         step = dot(jnp.concatenate([state, state, state], axis=1), hw[...])
         flow[0] += step[:, :CH]
         flow[1] += step[:, CH:]
+        if it < 2:
+            own_gates(state)
 
     lane = lax.broadcasted_iota(jnp.int32, (TOKENS, CH), 1)
     both = jnp.where(lane == 0, flow[0], flow[1])

time: 52.2 us -> 49.5 us (0.948)
  Pallas kernels: 48.5 us -> 45.9 us
    pallas_call x1, Pallas kernels: 48.5 us -> 45.9 us  [on_device(): pl.pallas_call(functools.partial(kernel, n_rows), out_shape=(jax.ShapeDty...]
where the time goes in v3:
time: 49.5 us; the launch traced here: 49.4 us
  Pallas kernels  45.9 us (93%)
  local copies, waits for them, and re-layouts  2.86 us (6%)
  between operations  0.64 us (1%)
    pallas_call x1, Pallas kernels, on_device(): pl.pallas_call(functools.partial(kernel, n_rows), out_shape=(jax.ShapeDty...  45.9 us
    unnamed x2, local copies, waits for them, and re-layouts  2.86 us

profile of v3, /device:TPU:25, one launch (start us, length us, event | category | flops | bytes accessed | tf_op | source)
XLA Modules:
  0.0 49.4 jit_solution(9660182476425344116)
XLA Ops:
  0.6 45.9 %shard_map.104 = (f32[2,8,64]{2,1,0:T(8,128)}, bf16[8,64,128]{2,1,0:T(8,128)(2,1)}) custom-call(bf16[8,64,128]{2,1,0:T(8,128)(2,1)} %frames_in.1, s32[1,3]{1,0:T(1,128)} %window.1, bf16[64,128]{1,0:T(8,128)(2,1)} %patch_in.1, bf16[9,128,128]{2,1,0:T(8,128)(2,1)} %dil_in.1, bf16[128,384]{1,0:T(8,128)(2,1)} %ctx_in.1, bf16[9,128,256]{2,1,0:T(8,128)(2,1)} %gate_in.1, ...), custom_call_target="tpu_custom_call" | custom-call | tf_op jit(solution)/shard_map/pallas_call | solution.py:610
  46.5 1.3 %copy.13 = f32[2,8,64]{2,1,0:T(8,128)} copy(f32[2,8,64]{2,1,0:T(8,128)} %get-tuple-element.4) | data formatting | bytes 8192
  47.8 1.6 %copy.14 = bf16[8,64,128]{2,1,0:T(8,128)(2,1)} copy(bf16[8,64,128]{2,1,0:T(8,128)(2,1)} %get-tuple-element.5) | data formatting | bytes 262144
